TPU v7x, 256 devices: a whole 4x4x8 slice. The times are simulated.
256 devices in a mesh: vox: 64 (over z, x, core), chan: 4 (over y).
Axes of the slice: x: 4, y: 4, z: 8, core: 2. Of those that a mesh axis runs over, the one named last changes fastest.
Arguments:
- model_blocks: bfloat16 [23552, 128, 128], P(('vox', 'chan')), may hold values from -0.15625 to 0.15625
- start_image: float32 [2048, 32, 128], P('vox'), may hold values from 0 to 2
- measured: float32 [2048, 32, 128], P(('vox', 'chan')), may hold values from -6 to 6
- step_size: float32 [32], replicated, may hold values from 0.05 to 0.25
- sent_tiles: int32 [64, 64, 4], P('vox'), may hold values from -1 to 31, as said below
- block_rows: int32 [23552], P(('vox', 'chan')), may hold values from 0 to 7
- block_slots: int32 [23552], P(('vox', 'chan')), may hold values from 0 to 255, as said below
Outputs:
- estimate: float32 [2048, 32, 128], P('vox')
- residual: float32 [2048, 32, 128], P(('vox', 'chan'))
Inputs may be any that keep to these rules, and one draw needn't show every extreme that they name: `sent_tiles`: an entry is -1 for an unused slot, else a tile of slab j; the used slots of one pair (j, v) come first, hold distinct tiles, number 1 to 4, and slab v always uses all 4 slots for itself. `block_slots`: every block names a used slot of its own device's vox index v, that is sent_tiles[j, v, s] is not -1.
All inputs are finite; a program needn't handle non-finite values.
Results may differ from a plain program's by a relative error of at most 0.0045.
Values may be sent and summed in bfloat16 or wider, within the bound.
A program may use at most 64 MiB of HBM per device.

v0:
```python
import jax
import jax.numpy as jnp
from jax import lax
from jax.sharding import PartitionSpec as P

ITERATIONS = 4


def shards(model_blocks, start_image, measured, step_size, sent_tiles, block_rows, block_slots):
    vox_count = lax.axis_size("vox")
    send_table = sent_tiles[0]
    capacity = send_table.shape[1]
    tile_count = start_image.shape[0]
    wave_count = start_image.shape[1]
    block_width = start_image.shape[2]
    row_count = measured.shape[0]
    block_count = model_blocks.shape[0]
    row_hot = (block_rows[None, :] == jnp.arange(row_count, dtype=jnp.int32)[:, None]).astype(
        jnp.float32
    )
    slot_hot = (
        block_slots[None, :] == jnp.arange(vox_count * capacity, dtype=jnp.int32)[:, None]
    ).astype(jnp.float32)
    tile_range = jnp.arange(tile_count, dtype=jnp.int32)[:, None]
    return_hot = (send_table.reshape(1, -1) == tile_range).astype(jnp.float32)
    step_gains = step_size[None, :, None]
    estimate = start_image
    residual = measured
    for iteration in range(ITERATIONS):
        rounded = estimate.astype(jnp.bfloat16)
        outgoing = jnp.take(rounded, jnp.maximum(send_table, 0), axis=0)
        arrived = lax.all_to_all(outgoing, "vox", split_axis=0, concat_axis=0, tiled=True)
        flat_tiles = arrived.reshape(vox_count * capacity, wave_count, block_width)
        forward_picked = jnp.take(flat_tiles, block_slots, axis=0)
        products = jnp.einsum(
            "bwv,bsv->bws", forward_picked, model_blocks, preferred_element_type=jnp.float32
        )
        summed = jnp.dot(
            row_hot,
            products.reshape(block_count, wave_count * block_width),
            precision=lax.Precision.HIGHEST,
        )
        residual = measured - summed.reshape(row_count, wave_count, block_width)
        narrow = residual.astype(jnp.bfloat16)
        picked = jnp.take(narrow, block_rows, axis=0)
        adjoint_terms = jnp.einsum(
            "bws,bsv->bwv", picked, model_blocks, preferred_element_type=jnp.float32
        )
        slot_sums = jnp.dot(
            slot_hot,
            adjoint_terms.reshape(block_count, wave_count * block_width),
            precision=lax.Precision.HIGHEST,
        )
        slot_sums = slot_sums.reshape(vox_count, capacity, wave_count, block_width)
        returned = lax.all_to_all(slot_sums, "vox", split_axis=0, concat_axis=0, tiled=True)
        local_sum = jnp.dot(
            return_hot,
            returned.reshape(-1, wave_count * block_width),
            precision=lax.Precision.HIGHEST,
        )
        slab_total = lax.psum(local_sum, "chan")
        estimate = jnp.maximum(
            estimate + step_gains * slab_total.reshape(tile_count, wave_count, block_width), 0.0
        )
    return (estimate, residual)


def solution(mesh):
    in_specs = (
        P(("vox", "chan"), None, None),
        P("vox", None, None),
        P(("vox", "chan"), None, None),
        P(),
        P("vox", None, None),
        P(("vox", "chan")),
        P(("vox", "chan")),
    )
    out_specs = (P("vox", None, None), P(("vox", "chan"), None, None))
    return jax.shard_map(shards, mesh=mesh, in_specs=in_specs, out_specs=out_specs, check_vma=False)
```

profile of v0, /device:TPU:1, one launch (start us, length us, event | category | flops | bytes accessed | tf_op | source)
XLA Modules:
  0.0 963.4 jit_solution(2402718531708179896)
XLA Ops:
  12.4 2.7 broadcast_select_fusion.3
  15.1 13.3 %all-to-all-start = ((bf16[64,4,32,128]{3,2,1,0:T(8,128)(2,1)}), bf16[64,4,32,128]{3,2,1,0:T(8,128)(2,1)}, u32[]{:S(2)}, u32[]{:S(2)}) async-start(bf16[64,4,32,128]{3,2,1,0:T(8,128)(2,1)} %broadcast_select_fusion.3), calls=%async_computation | async-start | bytes 4194304 | tf_op jit(solution)/shard_map/all_to_all | solution.py:32
  28.5 49.5 %all-to-all-done = bf16[64,4,32,128]{3,2,1,0:T(8,128)(2,1)} async-done(((bf16[64,4,32,128]{3,2,1,0:T(8,128)(2,1)}), bf16[64,4,32,128]{3,2,1,0:T(8,128)(2,1)}, u32[]{:S(2)}, u32[]{:S(2)}) %all-to-all-start) | async-done | bytes 2097184 | tf_op jit(solution)/shard_map/all_to_all | solution.py:32
  78.1 3.1 gather_fusion.1
  81.2 2.8 fusion.79
  90.2 2.6 fusion.18
  92.8 4.4 copy.71
  97.3 7.7 all-to-all-start.1
  105.2 94.4 %all-to-all-done.1 = f32[64,4,32,128]{3,2,1,0:T(8,128)} async-done(((f32[64,4,32,128]{3,2,1,0:T(8,128)}), f32[64,4,32,128]{3,2,1,0:T(8,128)}, u32[]{:S(2)}, u32[]{:S(2)}) %all-to-all-start.1) | async-done | bytes 4194336 | tf_op jit(solution)/shard_map/all_to_all | solution.py:55
  199.6 5.9 fusion.32
  206.5 43.8 %all-reduce.5.cloned.1.call-done = f32[32,32,128]{2,1,0:T(8,128)} async-done(((f32[32,32,128]{2,1,0:T(8,128)}), f32[32,32,128]{2,1,0:T(8,128)}) %all-reduce.5.cloned.1.call-update) | async-done | bytes 524304 | tf_op jit(solution)/shard_map/psum | solution.py:61
  255.6 62.5 %all_to_all.40 = bf16[64,4,32,128]{3,2,1,0:T(8,128)(2,1)} all-to-all(bf16[64,4,32,128]{3,2,1,0:T(8,128)(2,1)S(1)} %broadcast_select_fusion.2), channel_id=1, replica_groups=mesh['vox'=64,'chan'=4] {'vox'}, dimensions={0} | all-to-all | bytes 4194304 | tf_op jit(solution)/shard_map/all_to_all | solution.py:32
  318.1 3.1 gather_fusion.4
  321.2 2.8 fusion.75
  329.4 2.6 fusion.16
  334.5 101.8 %all_to_all.41 = f32[64,4,32,128]{3,2,1,0:T(8,128)S(1)} all-to-all(f32[64,4,32,128]{3,2,1,0:T(8,128)S(1)} %copy.78), channel_id=1, replica_groups=mesh['vox'=64,'chan'=4] {'vox'}, dimensions={0} | all-to-all | bytes 8388608 | tf_op jit(solution)/shard_map/all_to_all | solution.py:55
  436.3 3.9 fusion.35
  441.2 43.1 %all-reduce.7.cloned.1.call-done = f32[32,32,128]{2,1,0:T(8,128)} async-done(((f32[32,32,128]{2,1,0:T(8,128)}), f32[32,32,128]{2,1,0:T(8,128)}) %all-reduce.7.cloned.1.call-update) | async-done | bytes 524304 | tf_op jit(solution)/shard_map/psum | solution.py:61
  490.6 62.6 %all_to_all.42 = bf16[64,4,32,128]{3,2,1,0:T(8,128)(2,1)} all-to-all(bf16[64,4,32,128]{3,2,1,0:T(8,128)(2,1)S(1)} %broadcast_select_fusion.1), channel_id=1, replica_groups=mesh['vox'=64,'chan'=4] {'vox'}, dimensions={0} | all-to-all | bytes 4194304 | tf_op jit(solution)/shard_map/all_to_all | solution.py:32
  553.3 3.1 gather_fusion.7
  556.4 2.8 fusion.71
  564.6 2.6 fusion.14
  569.7 101.6 %all_to_all.43 = f32[64,4,32,128]{3,2,1,0:T(8,128)S(1)} all-to-all(f32[64,4,32,128]{3,2,1,0:T(8,128)S(1)} %copy.85), channel_id=1, replica_groups=mesh['vox'=64,'chan'=4] {'vox'}, dimensions={0} | all-to-all | bytes 8388608 | tf_op jit(solution)/shard_map/all_to_all | solution.py:55
  671.3 3.9 fusion.38
  676.2 43.1 %all-reduce.9.cloned.1.call-done = f32[32,32,128]{2,1,0:T(8,128)} async-done(((f32[32,32,128]{2,1,0:T(8,128)}), f32[32,32,128]{2,1,0:T(8,128)}) %all-reduce.9.cloned.1.call-update) | async-done | bytes 524304 | tf_op jit(solution)/shard_map/psum | solution.py:61
  724.6 62.7 %all_to_all.44 = bf16[64,4,32,128]{3,2,1,0:T(8,128)(2,1)} all-to-all(bf16[64,4,32,128]{3,2,1,0:T(8,128)(2,1)S(1)} %broadcast_select_fusion), channel_id=1, replica_groups=mesh['vox'=64,'chan'=4] {'vox'}, dimensions={0} | all-to-all | bytes 4194304 | tf_op jit(solution)/shard_map/all_to_all | solution.py:32
  787.3 3.1 gather_fusion.10
  790.5 2.8 fusion.67
  799.3 2.6 fusion.12
  804.4 101.7 %all_to_all.45 = f32[64,4,32,128]{3,2,1,0:T(8,128)S(1)} all-to-all(f32[64,4,32,128]{3,2,1,0:T(8,128)S(1)} %copy.92), channel_id=1, replica_groups=mesh['vox'=64,'chan'=4] {'vox'}, dimensions={0} | all-to-all | bytes 8388608 | tf_op jit(solution)/shard_map/all_to_all | solution.py:55
  906.1 3.9 fusion.41
  912.6 41.5 %all-reduce.11.cloned.1.call-done = f32[32,32,128]{2,1,0:T(8,128)} async-done(((f32[32,32,128]{2,1,0:T(8,128)}), f32[32,32,128]{2,1,0:T(8,128)}) %all-reduce.11.cloned.1.call-update) | async-done | bytes 524304 | tf_op jit(solution)/shard_map/psum | solution.py:61
  (81 shorter events, 60.2 us)
Async XLA Ops:
  7.2 74.0 %copy-start = (bf16[92,128,128]{2,1,0:T(8,128)(2,1)S(1)}, bf16[92,128,128]{2,1,0:T(8,128)(2,1)}, u32[]{:S(2)}) copy-start(bf16[92,128,128]{2,1,0:T(8,128)(2,1)} %param.13) | copy-start | bytes 9043972
  15.1 13.3 %copy-start.4 = (s32[92]{0:T(128)S(1)}, s32[92]{0:T(128)}, u32[]{:S(2)}) copy-start(s32[92]{0:T(128)} %param.19) | copy-start | bytes 1108
  15.1 13.4 %copy-start.6 = (s32[92]{0:T(128)S(1)}, s32[92]{0:T(128)}, u32[]{:S(2)}) copy-start(s32[92]{0:T(128)} %param.18) | copy-start | bytes 1108
  15.1 62.9 %all-to-all-start = ((bf16[64,4,32,128]{3,2,1,0:T(8,128)(2,1)}), bf16[64,4,32,128]{3,2,1,0:T(8,128)(2,1)}, u32[]{:S(2)}, u32[]{:S(2)}) async-start(bf16[64,4,32,128]{3,2,1,0:T(8,128)(2,1)} %broadcast_select_fusion.3), calls=%async_computation | async-start | bytes 4194304 | tf_op jit(solution)/shard_map/all_to_all | solution.py:32
  84.0 0.9 copy-start.2
  97.3 7.8 copy-start.3
  97.3 102.4 %all-to-all-start.1 = ((f32[64,4,32,128]{3,2,1,0:T(8,128)}), f32[64,4,32,128]{3,2,1,0:T(8,128)}, u32[]{:S(2)}, u32[]{:S(2)}) async-start(f32[64,4,32,128]{3,2,1,0:T(8,128)} %copy.71), calls=%async_computation.1 | async-start | bytes 8388608 | tf_op jit(solution)/shard_map/all_to_all | solution.py:55
  105.0 145.3 %all-reduce.5.cloned.1.call-start = ((), (), s32[]{:S(2)}) async-start(), calls=%async_computation.8 | async-start | bytes 1048576 | tf_op jit(solution)/shard_map/psum | solution.py:61
  199.6 50.6 %copy-start.5 = (f32[32]{0:T(128)S(1)}, f32[32]{0:T(128)}, u32[]{:S(2)}) copy-start(f32[32]{0:T(128)} %param.16) | copy-start | bytes 388
  206.4 277.9 %all-reduce.7.cloned.1.call-start = ((), (), s32[]{:S(2)}) async-start(), calls=%async_computation.9 | async-start | bytes 1048576 | tf_op jit(solution)/shard_map/psum | solution.py:61
  441.2 278.2 %all-reduce.9.cloned.1.call-start = ((), (), s32[]{:S(2)}) async-start(), calls=%async_computation.10 | async-start | bytes 1048576 | tf_op jit(solution)/shard_map/psum | solution.py:61
  676.2 277.9 %all-reduce.11.cloned.1.call-start = ((), (), s32[]{:S(2)}) async-start(), calls=%async_computation.11 | async-start | bytes 1048576 | tf_op jit(solution)/shard_map/psum | solution.py:61
  910.1 44.0 %copy-start.1 = (f32[32,32,128]{2,1,0:T(8,128)S(1)}, f32[32,32,128]{2,1,0:T(8,128)}, u32[]{:S(2)}) copy-start(f32[32,32,128]{2,1,0:T(8,128)} %get-tuple-element.14) | copy-start | bytes 1572868
Sparse Core Ops, SparseCore 0:
  206.5 43.6 all-reduce.4
  441.3 42.9 all-reduce.6
  676.3 42.9 all-reduce.8
  911.1 42.9 all-reduce.10
where the time goes:
time: 974 us; the launch traced here: 963 us
  blocking collectives  493 us (51%)
  waiting for transfers between devices  315 us (32%)
  matrix products  54.4 us (6%)
  local copies, waits for them, and re-layouts  46.8 us (5%)
  starting transfers between devices  21.2 us (2%)
  other arithmetic  18.1 us (2%)
  between operations  14.6 us (1%)
    all_to_all x3, blocking collectives, shards(): lax.all_to_all(slot_sums, 'vox', split_axis=0, concat_axis=0, tiled=True)  305 us
    all_to_all x3, blocking collectives, shards(): lax.all_to_all(outgoing, 'vox', split_axis=0, concat_axis=0, tiled=True)  188 us
    psum x4, waiting for transfers between devices, shards(): slab_total = lax.psum(local_sum, 'chan')  171 us
    all_to_all x1, waiting for transfers between devices, shards(): lax.all_to_all(slot_sums, 'vox', split_axis=0, concat_axis=0, tiled=True)  94.4 us
    all_to_all x1, waiting for transfers between devices, shards(): lax.all_to_all(outgoing, 'vox', split_axis=0, concat_axis=0, tiled=True)  49.5 us
  transfers between devices with their start and end apart: 6, of which 6 were waited for; matrix products, arithmetic and copies ran while one was open for 0% of the time, Pallas kernels for 0%

commit v1 on v0

v1 whole, which is shorter than its diff:
```python
import functools

import jax
import jax.numpy as jnp
from jax import lax
from jax.experimental import pallas as pl
from jax.experimental.pallas import tpu as pltpu
from jax.sharding import PartitionSpec as P

ITERATIONS = 4
MESH = pl.DeviceIdType.MESH
VMEM = pl.BlockSpec(memory_space=pltpu.VMEM)
SMEM = pl.BlockSpec(memory_space=pltpu.SMEM)
ANY = pl.BlockSpec(memory_space=pl.ANY)


def exchange_body(vox, back, ahead, *refs):
    refs = list(refs)
    estimate_ref = refs.pop(0)
    if back:
        sums_ref, return_hot_ref, step_ref = refs.pop(0), refs.pop(0), refs.pop(0)
    if ahead:
        send_hot_ref = refs.pop(0)
    if back:
        new_estimate_ref = refs.pop(0)
    if ahead:
        arrived_ref = refs.pop(0)
    returned, outgoing, back_send, back_recv, out_send, out_recv = refs
    me = lax.axis_index("vox")
    barrier = pltpu.get_barrier_semaphore()

    def greet(step, carry):
        pl.semaphore_signal(
            barrier, inc=1, device_id={"vox": lax.rem(me + step, vox)}, device_id_type=MESH
        )
        return carry

    lax.fori_loop(1, vox, greet, 0)
    pl.semaphore_wait(barrier, vox - 1)

    def all_to_all(source, target, send_sem, recv_sem):
        def send(step, carry):
            peer = lax.rem(me + step, vox)
            pltpu.make_async_remote_copy(
                src_ref=source.at[peer],
                dst_ref=target.at[me],
                send_sem=send_sem,
                recv_sem=recv_sem,
                device_id={"vox": peer},
                device_id_type=MESH,
            ).start()
            return carry

        lax.fori_loop(1, vox, send, 0)
        target[me] = source[me]
        others = pl.ds(0, vox - 1)
        pltpu.make_async_copy(target.at[others], target.at[others], recv_sem).wait()
        pltpu.make_async_copy(source.at[others], source.at[others], send_sem).wait()

    estimate = estimate_ref[...]
    if back:
        all_to_all(sums_ref, returned, back_send, back_recv)
        gradient = jnp.dot(
            return_hot_ref[...],
            returned[...].reshape(-1, estimate.shape[-1]),
            preferred_element_type=jnp.float32,
        )
        estimate = jnp.maximum(estimate + step_ref[...] * gradient, 0.0)
        new_estimate_ref[...] = estimate
    if ahead:
        slots = jnp.dot(
            send_hot_ref[...], estimate.astype(jnp.bfloat16), preferred_element_type=jnp.float32
        )
        outgoing[...] = slots.astype(jnp.bfloat16).reshape(outgoing.shape)
        all_to_all(outgoing, arrived_ref, out_send, out_recv)


def exchange(vox, number, estimate, sums=None, return_hot=None, steps=None, send_hot=None):
    back, ahead = sums is not None, send_hot is not None
    width = estimate.shape[-1]
    packet = (vox, (return_hot if back else send_hot.T).shape[1] // vox, width)
    operands = [estimate]
    outs = []
    if back:
        operands += [sums, return_hot, steps]
        outs.append(jax.ShapeDtypeStruct(estimate.shape, jnp.float32))
    if ahead:
        operands.append(send_hot)
        outs.append(jax.ShapeDtypeStruct(packet, jnp.bfloat16))
    return pl.pallas_call(
        functools.partial(exchange_body, vox, back, ahead),
        out_shape=outs,
        in_specs=[VMEM] * len(operands),
        out_specs=[VMEM] * len(outs),
        scratch_shapes=[pltpu.VMEM(packet, jnp.bfloat16)] * 2 + [pltpu.SemaphoreType.DMA] * 4,
        compiler_params=pltpu.CompilerParams(
            collective_id=number, has_side_effects=True, vmem_limit_bytes=20 << 20
        ),
        name="exchange" + ("_back" if back else "") + ("_ahead" if ahead else ""),
    )(*operands)


def apply_body(sizes, unroll, *refs):
    count = len(sizes)
    slot_of, row_of, arrived_ref, measured_ref = refs[:4]
    models = refs[4 : 4 + count]
    sums_ref, residual_ref, tiles, held, predicted, narrow, sums, sems = refs[4 + count :]
    starts = [sum(sizes[:i]) for i in range(count)]
    copies = []
    for i, model in enumerate(models):
        copy = pltpu.make_async_copy(model, held.at[pl.ds(starts[i], sizes[i])], sems.at[i])
        copy.start()
        copies.append(copy)
    tiles[...] = arrived_ref[...].astype(jnp.float32).reshape(tiles.shape)
    sums[...] = jnp.zeros_like(sums)
    predicted[...] = jnp.zeros_like(predicted)
    for copy in copies:
        copy.wait()
    total = sum(sizes)

    def forward(step, carry):
        for u in range(unroll):
            k = (step * unroll + u) * 2
            left = jnp.concatenate([tiles[slot_of[k]], tiles[slot_of[k + 1]]], axis=0)
            right = held[pl.ds(k, 2)].reshape(2 * held.shape[1], held.shape[2])
            product = lax.dot_general(
                left.astype(jnp.bfloat16),
                right,
                (((1,), (1,)), ((), ())),
                preferred_element_type=jnp.float32,
            )
            half, width = tiles.shape[1], held.shape[1]
            predicted[row_of[k]] += product[:half, :width]
            predicted[row_of[k + 1]] += product[half:, width:]
        return carry

    lax.fori_loop(0, total // 2 // unroll, forward, 0)
    residual = measured_ref[...] - predicted[...]
    residual_ref[...] = residual
    narrow[...] = residual.astype(jnp.bfloat16).astype(jnp.float32)

    def adjoint(step, carry):
        for u in range(unroll):
            k = (step * unroll + u) * 2
            left = jnp.concatenate([narrow[row_of[k]], narrow[row_of[k + 1]]], axis=0)
            right = jnp.concatenate([held[k], held[k + 1]], axis=1)
            product = jnp.dot(left.astype(jnp.bfloat16), right, preferred_element_type=jnp.float32)
            half, width = tiles.shape[1], held.shape[2]
            sums[slot_of[k]] += product[:half, :width]
            sums[slot_of[k + 1]] += product[half:, width:]
        return carry

    lax.fori_loop(0, total // 2 // unroll, adjoint, 0)
    sums_ref[...] = sums[...].reshape(sums_ref.shape).astype(jnp.bfloat16)


def apply(slot_of, row_of, arrived, measured, models):
    sizes = [model.shape[0] for model in models]
    total = sum(sizes)
    block = models[0].shape[1:]
    waves, width = measured.shape[1:]
    slots = arrived.size // (waves * width)
    unroll = max(u for u in range(1, 24) if (total // 2) % u == 0)
    return pl.pallas_call(
        functools.partial(apply_body, sizes, unroll),
        out_shape=(
            jax.ShapeDtypeStruct(arrived.shape, jnp.bfloat16),
            jax.ShapeDtypeStruct(measured.shape, jnp.float32),
        ),
        in_specs=[SMEM, SMEM, VMEM, VMEM] + [ANY] * len(models),
        out_specs=(VMEM, VMEM),
        scratch_shapes=[
            pltpu.VMEM((slots, waves, width), jnp.float32),
            pltpu.VMEM((total,) + block, jnp.bfloat16),
            pltpu.VMEM(measured.shape, jnp.float32),
            pltpu.VMEM(measured.shape, jnp.float32),
            pltpu.VMEM((slots, waves, width), jnp.float32),
            pltpu.SemaphoreType.DMA((len(models),)),
        ],
        compiler_params=pltpu.CompilerParams(vmem_limit_bytes=40 << 20),
        name="apply_blocks",
    )(slot_of, row_of, arrived, measured, *models)


def shards(model_blocks, start_image, measured, step_size, sent_tiles, block_rows, block_slots):
    vox, chan = lax.axis_size("vox"), lax.axis_size("chan")
    channel = lax.axis_index("chan")
    send_table = sent_tiles[0]
    capacity = send_table.shape[1]
    tile_count, wave_count, width = start_image.shape
    row_count = measured.shape[0]
    waves = wave_count // chan

    def shift(value, by):
        return lax.ppermute(value, "chan", [(c, (c + by) % chan) for c in range(chan)])

    block_count = model_blocks.shape[0]
    half = block_count // 2
    from_left = shift(model_blocks, 1)
    from_right = shift(model_blocks, -1)
    far_low = shift(from_left[:half], 1)
    far_high = shift(from_right[half:], -1)
    models = [model_blocks, from_left, from_right, far_low, far_high]
    code = block_slots * row_count + block_rows
    codes = [code, shift(code, 1), shift(code, -1), shift(code, 2)]
    slot_of = jnp.concatenate([c // row_count for c in codes])
    row_of = jnp.concatenate([i * row_count + c % row_count for i, c in enumerate(codes)])
    quarters = measured.reshape(row_count, chan, waves, width)

    def quarter(by):
        return lax.dynamic_index_in_dim(quarters, (channel + by) % chan, axis=1, keepdims=False)

    group_measured = jnp.concatenate(
        [quarter(0), shift(quarter(1), 1), shift(quarter(-1), -1), shift(quarter(2), 2)]
    )

    estimate = lax.dynamic_slice_in_dim(start_image, channel * waves, waves, axis=1)
    estimate = estimate.reshape(tile_count * waves, width)
    steps = lax.dynamic_slice_in_dim(step_size, channel * waves, waves)
    steps = jnp.broadcast_to(jnp.tile(steps, tile_count)[:, None], estimate.shape)
    tile_of = jnp.repeat(jnp.arange(tile_count, dtype=jnp.int32), waves)
    wave_of = jnp.tile(jnp.arange(waves, dtype=jnp.int32), tile_count)
    slot_tile = jnp.repeat(send_table.reshape(-1), waves)
    slot_wave = jnp.tile(jnp.arange(waves, dtype=jnp.int32), vox * capacity)
    return_hot = (
        (tile_of[:, None] == slot_tile[None, :]) & (wave_of[:, None] == slot_wave[None, :])
    ).astype(jnp.bfloat16)
    send_hot = (
        (slot_tile[:, None] == tile_of[None, :]) & (slot_wave[:, None] == wave_of[None, :])
    ).astype(jnp.bfloat16)

    (arrived,) = exchange(vox, 0, estimate, send_hot=send_hot)
    for iteration in range(ITERATIONS):
        sums, residual = apply(slot_of, row_of, arrived, group_measured, models)
        if iteration < ITERATIONS - 1:
            estimate, arrived = exchange(vox, 1, estimate, sums, return_hot, steps, send_hot)
        else:
            (estimate,) = exchange(vox, 2, estimate, sums, return_hot, steps)

    parts = residual.reshape(chan, row_count, waves, width)
    own_rows = [parts[0], shift(parts[1], -1), shift(parts[3], 2), shift(parts[2], 1)]
    estimate = estimate.reshape(tile_count, waves, width)
    whole = [estimate] + [shift(estimate, -by) for by in range(1, chan)]

    def join(pieces):
        ordered = jnp.roll(jnp.stack(pieces, axis=1), channel, axis=1)
        return ordered.reshape(pieces[0].shape[0], chan * waves, width)

    return (join(whole), join(own_rows))


def solution(mesh):
    in_specs = (
        P(("vox", "chan"), None, None),
        P("vox", None, None),
        P(("vox", "chan"), None, None),
        P(),
        P("vox", None, None),
        P(("vox", "chan")),
        P(("vox", "chan")),
    )
    out_specs = (P("vox", None, None), P(("vox", "chan"), None, None))
    return jax.shard_map(shards, mesh=mesh, in_specs=in_specs, out_specs=out_specs, check_vma=False)
```

time: 974 us -> 321 us (0.33)
  blocking collectives: 493 us -> 0 us
  waiting for transfers between devices: 315 us -> 55.6 us
  Pallas kernels: 0 us -> 209 us
  matrix products: 54.4 us -> 0 us
  local copies, waits for them, and re-layouts: 46.8 us -> 23.4 us
  between operations: 14.6 us -> 0.93 us
    all_to_all x6 -> x0, blocking collectives: 493 us -> none  [the longest x3 305 us: shards(): lax.all_to_all(slot_sums, 'vox', split_axis=0, concat_axis=0, tiled=True)]
    pallas_call x0 -> x9, Pallas kernels: none -> 209 us  [the longest x5 163 us: exchange(): pl.pallas_call(functools.partial(exchange_body, vox, back, ahead), out_sh...]
    psum x4 -> x0, waiting for transfers between devices: 171 us -> none  [shards(): slab_total = lax.psum(local_sum, 'chan')]
    all_to_all x2 -> x0, waiting for transfers between devices: 144 us -> none  [the longest x1 94.4 us: shards(): lax.all_to_all(slot_sums, 'vox', split_axis=0, concat_axis=0, tiled=True)]
    ppermute x0 -> x16, waiting for transfers between devices: none -> 55.6 us  [shift(): lax.ppermute(value, 'chan', [(c, (c + by) % chan) for c in range(chan)])]
    dot_general x20 -> x0, matrix products: 54.4 us -> none  [the longest x4 17.7 us: shards(): jnp.dot(return_hot, returned.reshape(-1, wave_count * block_width), preci...]
    gather x12 -> x0, local copies, waits for them, and re-layouts: 27.6 us -> none  [the longest x4 12.6 us: shards(): forward_picked = jnp.take(flat_tiles, block_slots, axis=0)]
    all_to_all x2 -> x0, starting transfers between devices: 21 us -> none  [the longest x1 13.3 us: shards(): lax.all_to_all(outgoing, 'vox', split_axis=0, concat_axis=0, tiled=True)]
  transfers between devices with their start and end apart: 6 -> 16, of which waited for: 6 -> 5; matrix products, arithmetic and copies ran while one was open for 0% -> 9% of each run, Pallas kernels for 0% -> 8%
where the time goes in v1:
time: 321 us; the launch traced here: 319 us
  Pallas kernels  209 us (65%)
  waiting for transfers between devices  55.6 us (17%)
  local copies, waits for them, and re-layouts  23.4 us (7%)
  starting transfers between devices  18.7 us (6%)
  other arithmetic  10.9 us (3%)
    pallas_call x5, Pallas kernels, exchange(): pl.pallas_call(functools.partial(exchange_body, vox, back, ahead), out_sh...  163 us
    ppermute x16, waiting for transfers between devices, shift(): lax.ppermute(value, 'chan', [(c, (c + by) % chan) for c in range(chan)])  55.6 us
    pallas_call x4, Pallas kernels, apply(): pl.pallas_call(functools.partial(apply_body, sizes, unroll), out_shape=(j...  46.6 us
    ppermute x16, starting transfers between devices, shift(): lax.ppermute(value, 'chan', [(c, (c + by) % chan) for c in range(chan)])  18.7 us
    unnamed x35, local copies, waits for them, and re-layouts  7.32 us
  transfers between devices with their start and end apart: 16, of which 5 were waited for; matrix products, arithmetic and copies ran while one was open for 9% of the time, Pallas kernels for 8%

profile of v1, /device:TPU:1, one launch (start us, length us, event | category | flops | bytes accessed | tf_op | source)
XLA Modules:
  0.0 318.7 jit_solution(9159018567377624472)
XLA Ops:
  0.6 2.2 collective-permute-start.6
  2.8 1.5 collective-permute-start.7
  4.4 1.2 and_select_fusion.3
  5.6 1.6 collective-permute-start.2
  11.6 1.4 copy.14
  15.6 1.1 and_select_fusion.7
  16.8 3.0 and_convert_fusion.1.refs_1_.refs_4_
  19.8 47.8 %collective-permute-done.6.refs_5_ = bf16[92,128,128]{2,1,0:T(8,128)(2,1)S(1)} collective-permute-done((bf16[92,128,128]{2,1,0:T(8,128)(2,1)}, bf16[92,128,128]{2,1,0:T(8,128)(2,1)S(1)}, u32[]{:S(2)}, u32[]{:S(2)}) %collective-permute-start.6) | collective-permute-done | bytes 3014688 | tf_op jit(solution)/shard_map/ppermute | solution.py:195
  67.6 1.3 slice.28
  68.9 1.6 collective-permute-start.8
  70.5 2.8 slice.29
  73.3 1.6 collective-permute-start.9
  75.5 1.3 dynamic_slice.32
  76.8 1.4 dynamic-slice_bitcast_fusion.4
  78.3 2.0 and_convert_fusion.refs_2_
  81.7 1.2 copy-done.2
  83.8 26.7 %exchange_ahead.1.refs_2_ = bf16[64,32,128]{2,1,0:T(8,128)(2,1)S(1)} custom-call(f32[256,128]{1,0:T(8,128)S(1)} %copy-done.7, bf16[2048,256]{1,0:T(8,128)(2,1)S(1)} %copy-done.2), custom_call_target="tpu_custom_call" | custom-call | tf_op jit(solution)/shard_map/exchange_ahead/pallas_call | solution.py:90
  116.3 2.1 collective-permute-done.3
  119.2 1.8 copy-done.1
  122.1 11.8 %apply_blocks.4 = (bf16[64,32,128]{2,1,0:T(8,128)(2,1)S(1)}, f32[32,8,128]{2,1,0:T(8,128)}) custom-call(s32[368]{0:T(512)S(1)} %get-tuple-element.39.refs_0_, s32[368]{0:T(512)S(1)} %get-tuple-element.40.refs_1_, bf16[64,32,128]{2,1,0:T(8,128)(2,1)S(1)} %copy-done.6, f32[32,8,128]{2,1,0:T(8,128)S(1)} %pad_maximum_fusion.refs_3_, ...), custom_call_target="tpu_custom_call" | custom-call | tf_op jit(solution)/shard_map/apply_blocks/pallas_call | solution.py:164
  134.0 38.8 %exchange_back_ahead.3 = (f32[256,128]{1,0:T(8,128)S(1)}, bf16[64,32,128]{2,1,0:T(8,128)(2,1)S(1)}) custom-call(f32[256,128]{1,0:T(8,128)S(1)} %copy-done.8, bf16[64,32,128]{2,1,0:T(8,128)(2,1)S(1)} %get-tuple-element.13.refs_1_, bf16[256,2048]{1,0:T(8,128)(2,1)S(1)} %copy-done.4, f32[256,128]{1,0:T(8,128)S(1)} %broadcast_in_dim.18.refs_3_, ...), custom_call_target="tpu_custom_call" | custom-call | tf_op jit(solution)/shard_map/exchange_back_ahead/pallas_call | solution.py:90
  172.8 11.8 %apply_blocks.5 = (bf16[64,32,128]{2,1,0:T(8,128)(2,1)S(1)}, f32[32,8,128]{2,1,0:T(8,128)}) custom-call(s32[368]{0:T(512)S(1)} %get-tuple-element.39.refs_0_, s32[368]{0:T(512)S(1)} %get-tuple-element.40.refs_1_, bf16[64,32,128]{2,1,0:T(8,128)(2,1)S(1)} %get-tuple-element.15.refs_2_, f32[32,8,128]{2,1,0:T(8,128)S(1)} %pad_maximum_fusion.refs_3_, ...), custom_call_target="tpu_custom_call" | custom-call | tf_op jit(solution)/shard_map/apply_blocks/pallas_call | solution.py:164
  184.6 37.5 %exchange_back_ahead.4 = (f32[256,128]{1,0:T(8,128)S(1)}, bf16[64,32,128]{2,1,0:T(8,128)(2,1)S(1)}) custom-call(f32[256,128]{1,0:T(8,128)S(1)} %get-tuple-element.14.refs_0_, bf16[64,32,128]{2,1,0:T(8,128)(2,1)S(1)} %get-tuple-element.16.refs_1_, bf16[256,2048]{1,0:T(8,128)(2,1)S(1)} %copy-done.4, f32[256,128]{1,0:T(8,128)S(1)} %broadcast_in_dim.18.refs_3_, ...), custom_call_target="tpu_custom_call" | custom-call | tf_op jit(solution)/shard_map/exchange_back_ahead/pallas_call | solution.py:90
  222.2 11.8 %apply_blocks.6 = (bf16[64,32,128]{2,1,0:T(8,128)(2,1)S(1)}, f32[32,8,128]{2,1,0:T(8,128)}) custom-call(s32[368]{0:T(512)S(1)} %get-tuple-element.39.refs_0_, s32[368]{0:T(512)S(1)} %get-tuple-element.40.refs_1_, bf16[64,32,128]{2,1,0:T(8,128)(2,1)S(1)} %get-tuple-element.18.refs_2_, f32[32,8,128]{2,1,0:T(8,128)S(1)} %pad_maximum_fusion.refs_3_, ...), custom_call_target="tpu_custom_call" | custom-call | tf_op jit(solution)/shard_map/apply_blocks/pallas_call | solution.py:164
  234.0 37.5 %exchange_back_ahead.5 = (f32[256,128]{1,0:T(8,128)S(1)}, bf16[64,32,128]{2,1,0:T(8,128)(2,1)S(1)}) custom-call(f32[256,128]{1,0:T(8,128)S(1)} %get-tuple-element.17.refs_0_, bf16[64,32,128]{2,1,0:T(8,128)(2,1)S(1)} %get-tuple-element.19.refs_1_, bf16[256,2048]{1,0:T(8,128)(2,1)S(1)} %copy-done.4, f32[256,128]{1,0:T(8,128)S(1)} %broadcast_in_dim.18.refs_3_, ...), custom_call_target="tpu_custom_call" | custom-call | tf_op jit(solution)/shard_map/exchange_back_ahead/pallas_call | solution.py:90
  271.4 11.2 %apply_blocks.7 = (bf16[64,32,128]{2,1,0:T(8,128)(2,1)S(1)}, f32[32,8,128]{2,1,0:T(8,128)S(1)}) custom-call(s32[368]{0:T(512)S(1)} %get-tuple-element.39.refs_0_, s32[368]{0:T(512)S(1)} %get-tuple-element.40.refs_1_, bf16[64,32,128]{2,1,0:T(8,128)(2,1)S(1)} %get-tuple-element.21.refs_2_, f32[32,8,128]{2,1,0:T(8,128)S(1)} %pad_maximum_fusion.refs_3_, ...), custom_call_target="tpu_custom_call" | custom-call | tf_op jit(solution)/shard_map/apply_blocks/pallas_call | solution.py:164
  282.7 22.0 %exchange_back.1 = f32[256,128]{1,0:T(8,128)S(1)} custom-call(f32[256,128]{1,0:T(8,128)S(1)} %get-tuple-element.20.refs_0_, bf16[64,32,128]{2,1,0:T(8,128)(2,1)S(1)} %get-tuple-element.22.refs_1_, bf16[256,2048]{1,0:T(8,128)(2,1)S(1)} %copy-done.4, f32[256,128]{1,0:T(8,128)S(1)} %broadcast_in_dim.18.refs_3_), custom_call_target="tpu_custom_call" | custom-call | tf_op jit(solution)/shard_map/exchange_back/pallas_call | solution.py:90
  306.3 2.5 collective-permute-start.13
  308.8 1.3 collective-permute-start.14
  310.2 2.8 collective-permute-done.13
  312.9 1.0 collective-permute-start.15
  314.7 2.2 collective-permute-done.15
  (75 shorter events, 21.7 us)
Async XLA Ops:
  0.6 74.2 %copy-start = (f32[32,32,128]{2,1,0:T(8,128)S(1)}, f32[32,32,128]{2,1,0:T(8,128)}, u32[]{:S(2)}) copy-start(f32[32,32,128]{2,1,0:T(8,128)} %param.8) | copy-start | bytes 1572868
  0.6 66.9 %collective-permute-start.6 = (bf16[92,128,128]{2,1,0:T(8,128)(2,1)}, bf16[92,128,128]{2,1,0:T(8,128)(2,1)S(1)}, u32[]{:S(2)}, u32[]{:S(2)}) collective-permute-start(bf16[92,128,128]{2,1,0:T(8,128)(2,1)} %refs_4_.7), channel_id=1, source_target_pairs={{0,1},{1,2},{2,3},{3,0},{4,5},{5,6},{6,7},{7,4},{8,9},{9,10},{10,1... | collective-permute-start | bytes 9043976 | tf_op jit(solution)/shard_map/ppermute | solution.py:195
  2.8 67.7 %collective-permute-start.7 = (bf16[92,128,128]{2,1,0:T(8,128)(2,1)}, bf16[92,128,128]{2,1,0:T(8,128)(2,1)}, u32[]{:S(2)}, u32[]{:S(2)}) collective-permute-start(bf16[92,128,128]{2,1,0:T(8,128)(2,1)} %refs_4_.7), channel_id=1, source_target_pairs={{0,3},{1,0},{2,1},{3,2},{4,7},{5,4},{6,5},{7,6},{8,11},{9,8},{10,9... | collective-permute-start | bytes 9043976 | tf_op jit(solution)/shard_map/ppermute | solution.py:195
  5.6 105.7 %collective-permute-start.2 = (s32[92]{0:T(128)}, s32[92]{0:T(128)}, u32[]{:S(2)}, u32[]{:S(2)}) collective-permute-start(s32[92]{0:T(128)} %get-tuple-element.25), channel_id=1, source_target_pairs={{0,2},{1,3},{2,0},{3,1},{4,6},{5,7},{6,4},{7,5},{8,10},{9,11},{10,... | collective-permute-start | bytes 1112 | tf_op jit(solution)/shard_map/ppermute | solution.py:195
  7.1 105.2 %collective-permute-start.1 = (s32[92]{0:T(128)}, s32[92]{0:T(128)}, u32[]{:S(2)}, u32[]{:S(2)}) collective-permute-start(s32[92]{0:T(128)} %get-tuple-element.25), channel_id=1, source_target_pairs={{0,3},{1,0},{2,1},{3,2},{4,7},{5,4},{6,5},{7,6},{8,11},{9,8},{10,9... | collective-permute-start | bytes 1112 | tf_op jit(solution)/shard_map/ppermute | solution.py:195
  7.9 106.0 %collective-permute-start = (s32[92]{0:T(128)}, s32[92]{0:T(128)}, u32[]{:S(2)}, u32[]{:S(2)}) collective-permute-start(s32[92]{0:T(128)} %get-tuple-element.25), channel_id=1, source_target_pairs={{0,1},{1,2},{2,3},{3,0},{4,5},{5,6},{6,7},{7,4},{8,9},{9,10},{10,1... | collective-permute-start | bytes 1112 | tf_op jit(solution)/shard_map/ppermute | solution.py:195
  68.9 50.3 %collective-permute-start.8 = (bf16[46,128,128]{2,1,0:T(8,128)(2,1)}, bf16[46,128,128]{2,1,0:T(8,128)(2,1)}, u32[]{:S(2)}, u32[]{:S(2)}) collective-permute-start(bf16[46,128,128]{2,1,0:T(8,128)(2,1)} %slice.28), channel_id=1, source_target_pairs={{0,1},{1,2},{2,3},{3,0},{4,5},{5,6},{6,7},{7,4},{8,9},{9,10},{10,1... | collective-permute-start | bytes 4521992 | tf_op jit(solution)/shard_map/ppermute | solution.py:195
  73.3 45.9 %collective-permute-start.9 = (bf16[46,128,128]{2,1,0:T(8,128)(2,1)}, bf16[46,128,128]{2,1,0:T(8,128)(2,1)}, u32[]{:S(2)}, u32[]{:S(2)}) collective-permute-start(bf16[46,128,128]{2,1,0:T(8,128)(2,1)} %slice.29), channel_id=1, source_target_pairs={{0,3},{1,0},{2,1},{3,2},{4,7},{5,4},{6,5},{7,6},{8,11},{9,8},{10,9... | collective-permute-start | bytes 4521992 | tf_op jit(solution)/shard_map/ppermute | solution.py:195
  81.7 1.2 copy-start.2
  82.9 0.9 copy-start.7
  110.5 0.8 copy-start.5
  111.3 5.0 %collective-permute-start.5 = (f32[8,8,128]{2,1,0:T(8,128)}, f32[8,8,128]{2,1,0:T(8,128)S(1)}, u32[]{:S(2)}, u32[]{:S(2)}) collective-permute-start(f32[8,8,128]{2,1,0:T(8,128)} %get-tuple-element.32), channel_id=1, source_target_pairs={{0,2},{1,3},{2,0},{3,1},{4,6},{5,7},{6,4},{7,5},{8,10},{9,11},{10,... | collective-permute-start | bytes 98312 | tf_op jit(solution)/shard_map/ppermute | solution.py:195
  112.4 3.9 %collective-permute-start.4 = (f32[8,8,128]{2,1,0:T(8,128)}, f32[8,8,128]{2,1,0:T(8,128)S(1)}, u32[]{:S(2)}, u32[]{:S(2)}) collective-permute-start(f32[8,8,128]{2,1,0:T(8,128)} %get-tuple-element.30), channel_id=1, source_target_pairs={{0,3},{1,0},{2,1},{3,2},{4,7},{5,4},{6,5},{7,6},{8,11},{9,8},{10,9... | collective-permute-start | bytes 98312 | tf_op jit(solution)/shard_map/ppermute | solution.py:195
  113.9 4.4 %collective-permute-start.3 = (f32[8,8,128]{2,1,0:T(8,128)}, f32[8,8,128]{2,1,0:T(8,128)S(1)}, u32[]{:S(2)}, u32[]{:S(2)}) collective-permute-start(f32[8,8,128]{2,1,0:T(8,128)} %get-tuple-element.31), channel_id=1, source_target_pairs={{0,1},{1,2},{2,3},{3,0},{4,5},{5,6},{6,7},{7,4},{8,9},{9,10},{10,1... | collective-permute-start | bytes 98312 | tf_op jit(solution)/shard_map/ppermute | solution.py:195
  119.1 1.9 copy-start.1
  121.0 1.0 copy-start.6
  122.0 11.8 %copy-start.9 = (f32[256]{0:T(256)S(1)}, f32[256]{0:T(256)}, u32[]{:S(2)}) copy-start(f32[256]{0:T(256)} %broadcast_in_dim.17) | copy-start | bytes 3076
  122.0 11.9 %copy-start.3 = (bf16[2048,256]{1,0:T(8,128)(2,1)S(1)}, bf16[2048,256]{1,0:T(8,128)(2,1)}, u32[]{:S(2)}) copy-start(bf16[2048,256]{1,0:T(8,128)(2,1)} %and_convert_fusion.1.refs_1_.refs_4_) | copy-start | bytes 3145732
  122.0 11.9 %copy-start.4 = (bf16[256,2048]{1,0:T(8,128)(2,1)S(1)}, bf16[256,2048]{1,0:T(8,128)(2,1)}, u32[]{:S(2)}) copy-start(bf16[256,2048]{1,0:T(8,128)(2,1)} %and_convert_fusion.refs_2_) | copy-start | bytes 3145732
  122.1 11.9 %copy-start.8 = (f32[256,128]{1,0:T(8,128)S(1)}, f32[256,128]{1,0:T(8,128)}, u32[]{:S(2)}) copy-start(f32[256,128]{1,0:T(8,128)} %dynamic-slice_bitcast_fusion.refs_0_) | copy-start | bytes 393220
  304.7 13.0 %collective-permute-start.10 = (f32[32,8,128]{2,1,0:T(8,128)S(1)}, f32[32,8,128]{2,1,0:T(8,128)S(1)}, u32[]{:S(2)}, u32[]{:S(2)}) collective-permute-start(f32[32,8,128]{2,1,0:T(8,128)S(1)} %bitcast.48), channel_id=1, source_target_pairs={{0,3},{1,0},{2,1},{3,2},{4,7},{5,4},{6,5},{7,6},{8,11},{9,8},{10,9... | collective-permute-start | bytes 393224 | tf_op jit(solution)/shard_map/ppermute | solution.py:195
  305.6 12.0 %collective-permute-start.11 = (f32[32,8,128]{2,1,0:T(8,128)S(1)}, f32[32,8,128]{2,1,0:T(8,128)S(1)}, u32[]{:S(2)}, u32[]{:S(2)}) collective-permute-start(f32[32,8,128]{2,1,0:T(8,128)S(1)} %bitcast.49), channel_id=1, source_target_pairs={{0,2},{1,3},{2,0},{3,1},{4,6},{5,7},{6,4},{7,5},{8,10},{9,11},{10,... | collective-permute-start | bytes 393224 | tf_op jit(solution)/shard_map/ppermute | solution.py:195
  306.1 11.6 %collective-permute-start.12 = (f32[32,8,128]{2,1,0:T(8,128)S(1)}, f32[32,8,128]{2,1,0:T(8,128)S(1)}, u32[]{:S(2)}, u32[]{:S(2)}) collective-permute-start(f32[32,8,128]{2,1,0:T(8,128)S(1)} %bitcast.50), channel_id=1, source_target_pairs={{0,1},{1,2},{2,3},{3,0},{4,5},{5,6},{6,7},{7,4},{8,9},{9,10},{10,1... | collective-permute-start | bytes 393224 | tf_op jit(solution)/shard_map/ppermute | solution.py:195
  306.3 6.6 %collective-permute-start.13 = (f32[8,8,128]{2,1,0:T(8,128)S(1)}, f32[8,8,128]{2,1,0:T(8,128)S(1)}, u32[]{:S(2)}, u32[]{:S(2)}) collective-permute-start(f32[8,8,128]{2,1,0:T(8,128)S(1)} %get-tuple-element.28), channel_id=1, source_target_pairs={{0,3},{1,0},{2,1},{3,2},{4,7},{5,4},{6,5},{7,6},{8,11},{9,8},{10,9... | collective-permute-start | bytes 98312 | tf_op jit(solution)/shard_map/ppermute | solution.py:195
  308.8 5.9 %collective-permute-start.14 = (f32[8,8,128]{2,1,0:T(8,128)S(1)}, f32[8,8,128]{2,1,0:T(8,128)S(1)}, u32[]{:S(2)}, u32[]{:S(2)}) collective-permute-start(f32[8,8,128]{2,1,0:T(8,128)S(1)} %get-tuple-element.27), channel_id=1, source_target_pairs={{0,2},{1,3},{2,0},{3,1},{4,6},{5,7},{6,4},{7,5},{8,10},{9,11},{10,... | collective-permute-start | bytes 98312 | tf_op jit(solution)/shard_map/ppermute | solution.py:195
  312.9 4.0 %collective-permute-start.15 = (f32[8,8,128]{2,1,0:T(8,128)S(1)}, f32[8,8,128]{2,1,0:T(8,128)S(1)}, u32[]{:S(2)}, u32[]{:S(2)}) collective-permute-start(f32[8,8,128]{2,1,0:T(8,128)S(1)} %get-tuple-element.26), channel_id=1, source_target_pairs={{0,1},{1,2},{2,3},{3,0},{4,5},{5,6},{6,7},{7,4},{8,9},{9,10},{10,1... | collective-permute-start | bytes 98312 | tf_op jit(solution)/shard_map/ppermute | solution.py:195

commit v2 on v0

v2 whole, which is shorter than its diff:
```python
import functools

import jax
import jax.numpy as jnp
from jax import lax
from jax.experimental import pallas as pl
from jax.experimental.pallas import tpu as pltpu
from jax.sharding import PartitionSpec as P

ITERATIONS = 4
STREAMS = 2
MESH = pl.DeviceIdType.MESH
VMEM = pl.BlockSpec(memory_space=pltpu.VMEM)
ANY = pl.BlockSpec(memory_space=pl.ANY)


def landweber_body(
    vox,
    chan,
    model_ref,
    gather_ref,
    scatter_ref,
    start_ref,
    measured_ref,
    steps_ref,
    send_hot_ref,
    return_hot_ref,
    row_hot_ref,
    row_sum_ref,
    estimate_out,
    residual_out,
    held,
    gather_hot,
    scatter_hot,
    estimate,
    outgoing,
    arrived,
    picked,
    tiles,
    high,
    low,
    narrow,
    terms,
    group_terms,
    slot_sums,
    returned,
    load_sems,
    ahead_send,
    ahead_recv,
    tile_send,
    tile_recv,
    term_send,
    term_recv,
    back_send,
    back_recv,
    final_send,
    final_recv,
):
    me, channel = lax.axis_index("vox"), lax.axis_index("chan")
    peers = range(1, chan)
    block_count, samples, voxels = held.shape
    rows = tiles.shape[2]
    waves = rows // block_count
    pack = 16 // waves
    f32, bf16 = jnp.float32, jnp.bfloat16

    def vox_peer(step):
        return lax.rem(me + step, vox)

    def chan_peer(step):
        return lax.rem(channel + step, chan)

    barrier = pltpu.get_barrier_semaphore()

    def greet(step, carry):
        pl.semaphore_signal(barrier, inc=1, device_id={"vox": vox_peer(step)}, device_id_type=MESH)
        return carry

    lax.fori_loop(1, vox, greet, 0)
    for p in peers:
        pl.semaphore_signal(barrier, inc=1, device_id={"chan": chan_peer(p)}, device_id_type=MESH)

    loads = [
        pltpu.make_async_copy(source, target, load_sems.at[i])
        for i, (source, target) in enumerate(
            [(gather_ref, gather_hot), (model_ref, held), (scatter_ref, scatter_hot)]
        )
    ]
    for load in loads:
        load.start()

    estimate[...] = start_ref[...]
    high[rows * chan :, :] = jnp.zeros_like(high[rows * chan :, :])
    low[rows * chan :, :] = jnp.zeros_like(low[rows * chan :, :])
    for p in range(chan):
        tail = group_terms.shape[2] - rows
        group_terms[:, p, rows:, :] = jnp.zeros((STREAMS, tail, voxels), bf16)

    def start_vox(source, target, send_sem, recv_sem, g):
        def send(step, carry):
            peer = vox_peer(step)
            pltpu.make_async_remote_copy(
                src_ref=source.at[g, peer],
                dst_ref=target.at[g, me],
                send_sem=send_sem.at[g],
                recv_sem=recv_sem.at[g],
                device_id={"vox": peer},
                device_id_type=MESH,
            ).start()
            return carry

        lax.fori_loop(1, vox, send, 0)
        target[g, me] = source[g, me]

    def wait_vox(source, target, send_sem, recv_sem, g):
        others = pl.ds(0, vox - 1)
        pltpu.make_async_copy(target.at[g, others], target.at[g, others], recv_sem.at[g]).wait()
        pltpu.make_async_copy(source.at[g, others], source.at[g, others], send_sem.at[g]).wait()

    def chan_copy(source, target, send_sem, recv_sem, g, p):
        return pltpu.make_async_remote_copy(
            src_ref=source.at[g, p],
            dst_ref=target.at[g, chan - p, pl.ds(0, rows)],
            send_sem=send_sem.at[g, p],
            recv_sem=recv_sem.at[g, chan - p],
            device_id={"chan": chan_peer(p)},
            device_id_type=MESH,
        )

    def wait_chan(source, target, send_sem, recv_sem, g):
        for p in peers:
            landed = target.at[g, p, pl.ds(0, rows)]
            pltpu.make_async_copy(landed, landed, recv_sem.at[g, p]).wait()
            pltpu.make_async_copy(source.at[g, p], source.at[g, p], send_sem.at[g, p]).wait()

    def start_ahead(g):
        slots = jnp.dot(
            send_hot_ref[...], estimate[g].astype(bf16), preferred_element_type=f32
        )
        outgoing[g] = slots.astype(bf16).reshape(outgoing.shape[1:])

    def send_ahead(g):
        start_vox(outgoing, arrived, ahead_send, ahead_recv, g)

    for g in range(STREAMS):
        start_ahead(g)
    pl.semaphore_wait(barrier, vox - 1 + chan - 1)
    for g in range(STREAMS):
        send_ahead(g)
    loads[0].wait()

    upper = lax.broadcasted_iota(jnp.int32, (8, voxels), 0) < waves

    def diagonal(product, p):
        base = 16 * p
        halves = []
        for h in range(2):
            part = slice(base + 8 * h, base + 8 * h + 8)
            first = product[part, (2 * h) * voxels : (2 * h + 1) * voxels]
            second = product[part, (2 * h + 1) * voxels : (2 * h + 2) * voxels]
            halves.append(jnp.where(upper, first, second))
        return jnp.concatenate(halves, axis=0)

    def pick_tiles(g, carry):
        wait_vox(outgoing, arrived, ahead_send, ahead_recv, g)
        source = arrived[g].reshape(-1, voxels)
        for p in list(peers) + [0]:
            part = jnp.dot(
                gather_hot[p * rows : (p + 1) * rows, :], source, preferred_element_type=f32
            ).astype(bf16)
            if p == 0:
                tiles[g, 0] = part
            else:
                picked[g, p] = part
                chan_copy(picked, tiles, tile_send, tile_recv, g, p).start()
        return carry

    def apply(g, carry):
        wait_chan(picked, tiles, tile_send, tile_recv, g)
        for q in range(block_count // pack):
            span = slice(16 * q, 16 * q + 16)
            left = jnp.concatenate([tiles[g, p, span, :] for p in range(chan)], axis=0)
            right = held[pack * q : pack * (q + 1)].reshape(pack * samples, voxels)
            product = lax.dot_general(
                left, right, (((1,), (1,)), ((), ())), preferred_element_type=f32
            )
            for p in range(chan):
                piece = diagonal(product, p)
                top = piece.astype(bf16)
                where = slice(p * rows + 16 * q, p * rows + 16 * q + 16)
                high[where, :] = top
                low[where, :] = (piece - top.astype(f32)).astype(bf16)
        predicted = jnp.dot(row_sum_ref[...], high[...], preferred_element_type=f32)
        predicted += jnp.dot(row_sum_ref[...], low[...], preferred_element_type=f32)
        part = predicted.shape[0] // chan
        residuals = []
        for p in range(chan):
            residual = measured_ref[chan_peer(p), g] - predicted[p * part : (p + 1) * part]
            residual_out[chan_peer(p), g] = residual
            residuals.append(residual.astype(bf16))
        narrow[...] = jnp.dot(
            row_hot_ref[...], jnp.concatenate(residuals, axis=0), preferred_element_type=f32
        ).astype(bf16)
        for q in range(block_count // pack):
            left = jnp.concatenate(
                [narrow[p * rows + 16 * q : p * rows + 16 * q + 16, :] for p in range(chan)], axis=0
            )
            right = jnp.concatenate([held[pack * q + i] for i in range(pack)], axis=1)
            product = jnp.dot(left, right, preferred_element_type=f32)
            for p in range(chan):
                piece = diagonal(product, p).astype(bf16)
                if p == 0:
                    group_terms[g, 0, 16 * q : 16 * q + 16, :] = piece
                else:
                    terms[g, p, 16 * q : 16 * q + 16, :] = piece
        for p in peers:
            chan_copy(terms, group_terms, term_send, term_recv, g, p).start()
        return carry

    def sum_slots(g, carry):
        wait_chan(terms, group_terms, term_send, term_recv, g)
        source = group_terms[g].reshape(-1, voxels)
        chunk = 256
        packets = chunk // slot_sums.shape[2]
        for i in range(scatter_hot.shape[0] // chunk):
            part = jnp.dot(
                scatter_hot[i * chunk : (i + 1) * chunk, :], source, preferred_element_type=f32
            )
            slot_sums[g, i * packets : (i + 1) * packets] = part.astype(bf16).reshape(
                (packets,) + slot_sums.shape[2:]
            )
        start_vox(slot_sums, returned, back_send, back_recv, g)
        return carry

    def update(g):
        wait_vox(slot_sums, returned, back_send, back_recv, g)
        gradient = jnp.dot(
            return_hot_ref[...], returned[g].reshape(-1, voxels), preferred_element_type=f32
        )
        estimate[g] = jnp.maximum(estimate[g] + steps_ref[g] * gradient, 0.0)

    def update_and_send(g, carry):
        update(g)
        start_ahead(g)
        send_ahead(g)
        return carry

    def iterate(iteration, carry):
        lax.fori_loop(0, STREAMS, pick_tiles, 0)

        @pl.when(iteration == 0)
        def _():
            for load in loads[1:]:
                load.wait()

        lax.fori_loop(0, STREAMS, apply, 0)
        lax.fori_loop(0, STREAMS, sum_slots, 0)

        @pl.when(iteration < ITERATIONS - 1)
        def _():
            lax.fori_loop(0, STREAMS, update_and_send, 0)

        return carry

    lax.fori_loop(0, ITERATIONS, iterate, 0)

    def final_copy(g, p):
        return pltpu.make_async_remote_copy(
            src_ref=estimate.at[g],
            dst_ref=estimate_out.at[channel, g],
            send_sem=final_send.at[g, p],
            recv_sem=final_recv.at[g, chan - p],
            device_id={"chan": chan_peer(p)},
            device_id_type=MESH,
        )

    for g in range(STREAMS):
        update(g)
        for p in peers:
            final_copy(g, p).start()
        estimate_out[channel, g] = estimate[g]
    for g in range(STREAMS):
        for p in peers:
            landed = estimate_out.at[chan_peer(p), g]
            pltpu.make_async_copy(landed, landed, final_recv.at[g, p]).wait()
            pltpu.make_async_copy(estimate.at[g], estimate.at[g], final_send.at[g, p]).wait()


def shards(model_blocks, start_image, measured, step_size, sent_tiles, block_rows, block_slots):
    vox, chan = lax.axis_size("vox"), lax.axis_size("chan")
    channel = lax.axis_index("chan")
    send_table = sent_tiles[0]
    capacity = send_table.shape[1]
    tile_count, wave_count, width = start_image.shape
    row_count, block_count = measured.shape[0], model_blocks.shape[0]
    waves = wave_count // chan // STREAMS
    slots = vox * capacity
    rows = block_count * waves
    padded = -(-rows // 128) * 128
    int32, bf16 = jnp.int32, jnp.bfloat16

    def shift(value, by):
        return lax.ppermute(value, "chan", [(c, (c + by) % chan) for c in range(chan)])

    def flat(index, minor):
        spread = index[..., None] * minor + jnp.arange(minor, dtype=int32)
        return jnp.where(index[..., None] < 0, -1, spread).reshape(index.shape[:-1] + (-1,))

    peer_slots = jnp.stack([block_slots] + [shift(block_slots, -p) for p in range(1, chan)])
    slot_code = flat(peer_slots, waves)
    gather_hot = (slot_code.reshape(-1)[:, None] == jnp.arange(slots * waves)[None, :]).astype(bf16)
    slot_code = jnp.pad(slot_code, ((0, 0), (0, padded - rows)), constant_values=-1)
    scatter_hot = (
        jnp.arange(slots * waves)[:, None] == slot_code.reshape(-1)[None, :]
    ).astype(bf16)
    send_code = flat(send_table.reshape(-1), waves)
    tile_range = jnp.arange(tile_count * waves)
    send_hot = (send_code[:, None] == tile_range[None, :]).astype(bf16)
    return_hot = (tile_range[:, None] == send_code[None, :]).astype(bf16)
    row_code = flat(
        jnp.arange(chan, dtype=int32)[:, None] * row_count + block_rows[None, :], waves
    ).reshape(-1)
    row_range = jnp.arange(chan * row_count * waves)
    row_hot = (row_code[:, None] == row_range[None, :]).astype(bf16)
    row_code = jnp.pad(row_code, (0, chan * (padded - rows)), constant_values=-1)
    row_sum = (row_range[:, None] == row_code[None, :]).astype(bf16)

    own = lax.dynamic_slice_in_dim(start_image, channel * waves * STREAMS, waves * STREAMS, axis=1)
    own = own.reshape(tile_count, STREAMS, waves, width).transpose(1, 0, 2, 3)
    own = own.reshape(STREAMS, tile_count * waves, width)
    steps = lax.dynamic_slice_in_dim(step_size, channel * waves * STREAMS, waves * STREAMS)
    steps = jnp.tile(steps.reshape(STREAMS, waves), (1, tile_count))
    steps = jnp.broadcast_to(steps[:, :, None], own.shape)
    split = measured.reshape(row_count, chan, STREAMS, waves, width).transpose(1, 2, 0, 3, 4)
    split = split.reshape(chan, STREAMS, row_count * waves, width)

    packet = (STREAMS, vox, capacity * waves, width)
    quarter = (STREAMS, chan, rows, width)
    dma = pltpu.SemaphoreType.DMA
    estimate, residual = pl.pallas_call(
        functools.partial(landweber_body, vox, chan),
        out_shape=(
            jax.ShapeDtypeStruct((chan,) + own.shape, jnp.float32),
            jax.ShapeDtypeStruct(split.shape, jnp.float32),
        ),
        in_specs=[ANY] * 3 + [VMEM] * 7,
        out_specs=(VMEM, VMEM),
        scratch_shapes=[
            pltpu.VMEM(model_blocks.shape, bf16),
            pltpu.VMEM(gather_hot.shape, bf16),
            pltpu.VMEM(scatter_hot.shape, bf16),
            pltpu.VMEM(own.shape, jnp.float32),
            pltpu.VMEM(packet, bf16),
            pltpu.VMEM(packet, bf16),
            pltpu.VMEM(quarter, bf16),
            pltpu.VMEM(quarter, bf16),
            pltpu.VMEM((chan * padded, width), bf16),
            pltpu.VMEM((chan * padded, width), bf16),
            pltpu.VMEM((chan * rows, width), bf16),
            pltpu.VMEM(quarter, bf16),
            pltpu.VMEM((STREAMS, chan, padded, width), bf16),
            pltpu.VMEM(packet, bf16),
            pltpu.VMEM(packet, bf16),
            dma((3,)),
            dma((STREAMS,)),
            dma((STREAMS,)),
            dma((STREAMS, chan)),
            dma((STREAMS, chan)),
            dma((STREAMS, chan)),
            dma((STREAMS, chan)),
            dma((STREAMS,)),
            dma((STREAMS,)),
            dma((STREAMS, chan)),
            dma((STREAMS, chan)),
        ],
        compiler_params=pltpu.CompilerParams(
            collective_id=0, has_side_effects=True, vmem_limit_bytes=32 << 20
        ),
        name="landweber",
    )(
        model_blocks,
        gather_hot,
        scatter_hot,
        own,
        split,
        steps,
        send_hot,
        return_hot,
        row_hot,
        row_sum,
    )
    estimate = estimate.reshape(chan, STREAMS, tile_count, waves, width).transpose(2, 0, 1, 3, 4)
    residual = residual.reshape(chan, STREAMS, row_count, waves, width).transpose(2, 0, 1, 3, 4)
    return (
        estimate.reshape(tile_count, wave_count, width),
        residual.reshape(row_count, wave_count, width),
    )


def solution(mesh):
    in_specs = (
        P(("vox", "chan"), None, None),
        P("vox", None, None),
        P(("vox", "chan"), None, None),
        P(),
        P("vox", None, None),
        P(("vox", "chan")),
        P(("vox", "chan")),
    )
    out_specs = (P("vox", None, None), P(("vox", "chan"), None, None))
    return jax.shard_map(shards, mesh=mesh, in_specs=in_specs, out_specs=out_specs, check_vma=False)
```

time: 974 us -> 198 us (0.20); the launches traced: 963 us -> 198 us
  blocking collectives: 493 us -> 0 us
  waiting for transfers between devices: 315 us -> 0.01 us
  Pallas kernels: 0 us -> 182 us
  matrix products: 54.4 us -> 0 us
  local copies, waits for them, and re-layouts: 46.8 us -> 4.3 us
  starting transfers between devices: 21.2 us -> 5.28 us
  between operations: 14.6 us -> 0.92 us
  other arithmetic: 18.1 us -> 5.73 us
    all_to_all x6 -> x0, blocking collectives: 493 us -> none  [the longest x3 305 us: shards(): lax.all_to_all(slot_sums, 'vox', split_axis=0, concat_axis=0, tiled=True)]
    pallas_call x0 -> x1, Pallas kernels: none -> 182 us  [shards(): pl.pallas_call(functools.partial(landweber_body, vox, chan), out_shape=(j...]
    psum x4 -> x0, waiting for transfers between devices: 171 us -> none  [shards(): slab_total = lax.psum(local_sum, 'chan')]
    all_to_all x2 -> x0, waiting for transfers between devices: 144 us -> none  [the longest x1 94.4 us: shards(): lax.all_to_all(slot_sums, 'vox', split_axis=0, concat_axis=0, tiled=True)]
    dot_general x20 -> x0, matrix products: 54.4 us -> none  [the longest x4 17.7 us: shards(): jnp.dot(return_hot, returned.reshape(-1, wave_count * block_width), preci...]
    gather x12 -> x0, local copies, waits for them, and re-layouts: 27.6 us -> none  [the longest x4 12.6 us: shards(): forward_picked = jnp.take(flat_tiles, block_slots, axis=0)]
    all_to_all x2 -> x0, starting transfers between devices: 21 us -> none  [the longest x1 13.3 us: shards(): lax.all_to_all(outgoing, 'vox', split_axis=0, concat_axis=0, tiled=True)]
    dot_general x12 -> x0, local copies, waits for them, and re-layouts: 12.7 us -> none  [the longest x8 12.2 us: shards(): jnp.dot(slot_hot, adjoint_terms.reshape(block_count, wave_count * block_w...]
  transfers between devices with their start and end apart: 6 -> 3, of which waited for: 6 -> 0; matrix products, arithmetic and copies ran while one was open for 0% -> 3% of each run, Pallas kernels for 0% -> 0%
where the time goes in v2:
time: 198 us
  Pallas kernels  182 us (92%)
  other arithmetic  5.73 us (3%)
  starting transfers between devices  5.28 us (3%)
  local copies, waits for them, and re-layouts  4.3 us (2%)
    pallas_call x1, Pallas kernels, shards(): pl.pallas_call(functools.partial(landweber_body, vox, chan), out_shape=(j...  182 us
    ppermute x3, starting transfers between devices, shift(): lax.ppermute(value, 'chan', [(c, (c + by) % chan) for c in range(chan)])  5.28 us
  transfers between devices with their start and end apart: 3, of which 0 were waited for; matrix products, arithmetic and copies ran while one was open for 3% of the time, Pallas kernels for 0%

profile of v2, /device:TPU:1, one launch (start us, length us, event | category | flops | bytes accessed | tf_op | source)
XLA Modules:
  0.0 197.9 jit_solution(17465284727447213910)
XLA Ops:
  0.7 3.6 %collective-permute-start = (s32[92]{0:T(128)}, s32[92]{0:T(128)S(1)}, u32[]{:S(2)}, u32[]{:S(2)}) collective-permute-start(s32[92]{0:T(128)} %param.13), channel_id=1, source_target_pairs={{0,3},{1,0},{2,1},{3,2},{4,7},{5,4},{6,5},{7,6},{8,11},{9,8},{10,9... | collective-permute-start | bytes 1112 | tf_op jit(solution)/shard_map/ppermute | solution.py:303
  4.3 1.6 collective-permute-start.1
  5.9 0.7 add_compare_fusion
  6.7 0.7 add_multiply_fusion
  7.4 0.7 broadcast_compare_fusion
  8.1 0.7 broadcast_multiply_fusion
  8.8 0.1 copy.15
  8.9 0.1 lt.38
  9.0 0.1 copy.16
  9.1 0.1 mul.48
  9.2 0.1 add_select_fusion.2
  9.4 0.1 select_n.49
  9.5 0.2 fusion.4.send_hot_ref
  9.7 0.7 dynamic_slice.7
  10.6 0.1 tile.11
  10.7 0.2 add_select_fusion
  10.9 0.1 select_n.51
  11.0 0.3 fusion.3.row_hot_ref
  11.4 0.1 add.103
  11.6 0.1 copy.13
  11.8 0.1 broadcast_in_dim.55
  11.9 0.2 broadcast_in_dim.57
  12.0 0.2 add_select_fusion.1
  12.2 0.1 select_n.45
  12.4 0.1 add.98
  12.5 0.1 add.101
  12.7 0.6 fusion.1.gather_ref
  13.2 1.3 fusion.scatter_ref
  14.5 0.1 broadcast_in_dim.59.steps_ref
  14.6 181.7 %landweber.1 = (f32[4,2,128,128]{3,2,1,0:T(8,128)S(1)}, f32[4,2,32,128]{3,2,1,0:T(8,128)S(1)}) custom-call(bf16[92,128,128]{2,1,0:T(8,128)(2,1)S(1)} %copy-done.1, bf16[1472,1024]{1,0:T(8,128)(2,1)S(1)} %fusion.1.gather_ref, bf16[1024,1536]{1,0:T(8,128)(2,1)S(1)} %fusion.scatter_ref, f32[2,128,128]{2,1,0:T(8,128)S(1)} %bitcast.20, ...), custom_call_target="tpu_custom_call" | custom-call | tf_op jit(solution)/shard_map/landweber/pallas_call | solution.py:340
  196.3 0.9 copy.17
  197.2 0.7 copy.18
  (27 shorter events, 0.4 us)
Async XLA Ops:
  0.6 10.1 %copy-start = (f32[32,32,128]{2,1,0:T(8,128)S(1)}, f32[32,32,128]{2,1,0:T(8,128)}, u32[]{:S(2)}) copy-start(f32[32,32,128]{2,1,0:T(8,128)} %param.8) | copy-start | bytes 1572868
  0.6 11.1 %copy-start.3 = (s32[92]{0:T(128)S(1)}, s32[92]{0:T(128)}, u32[]{:S(2)}) copy-start(s32[92]{0:T(128)} %param.13) | copy-start | bytes 1108
  0.7 11.0 %copy-start.2 = (f32[8,32,128]{2,1,0:T(8,128)S(1)}, f32[8,32,128]{2,1,0:T(8,128)}, u32[]{:S(2)}) copy-start(f32[8,32,128]{2,1,0:T(8,128)} %param.9) | copy-start | bytes 393220
  0.7 11.0 %collective-permute-start = (s32[92]{0:T(128)}, s32[92]{0:T(128)S(1)}, u32[]{:S(2)}, u32[]{:S(2)}) collective-permute-start(s32[92]{0:T(128)} %param.13), channel_id=1, source_target_pairs={{0,3},{1,0},{2,1},{3,2},{4,7},{5,4},{6,5},{7,6},{8,11},{9,8},{10,9... | collective-permute-start | bytes 1112 | tf_op jit(solution)/shard_map/ppermute | solution.py:303
  4.3 7.4 %collective-permute-start.2 = (s32[92]{0:T(128)}, s32[92]{0:T(128)S(1)}, u32[]{:S(2)}, u32[]{:S(2)}) collective-permute-start(s32[92]{0:T(128)} %param.13), channel_id=1, source_target_pairs={{0,1},{1,2},{2,3},{3,0},{4,5},{5,6},{6,7},{7,4},{8,9},{9,10},{10,1... | collective-permute-start | bytes 1112 | tf_op jit(solution)/shard_map/ppermute | solution.py:303
  4.3 7.4 %collective-permute-start.1 = (s32[92]{0:T(128)}, s32[92]{0:T(128)S(1)}, u32[]{:S(2)}, u32[]{:S(2)}) collective-permute-start(s32[92]{0:T(128)} %param.13), channel_id=1, source_target_pairs={{0,2},{1,3},{2,0},{3,1},{4,6},{5,7},{6,4},{7,5},{8,10},{9,11},{10,... | collective-permute-start | bytes 1112 | tf_op jit(solution)/shard_map/ppermute | solution.py:303
  12.7 1.9 copy-start.1

commit v3 on v2

v3 whole, which is shorter than its diff:
```python
import functools

import jax
import jax.numpy as jnp
from jax import lax
from jax.experimental import pallas as pl
from jax.experimental.pallas import tpu as pltpu
from jax.sharding import PartitionSpec as P

ITERATIONS = 4
STREAMS = 2
PLANE = 8
LANES = 128
MESH = pl.DeviceIdType.MESH
VMEM = pl.BlockSpec(memory_space=pltpu.VMEM)
ANY = pl.BlockSpec(memory_space=pl.ANY)


def landweber_body(
    vox,
    chan,
    model_ref,
    slots_ref,
    start_ref,
    measured_ref,
    steps_ref,
    send_hot_ref,
    return_hot_ref,
    row_hot_ref,
    row_sum_ref,
    estimate_out,
    residual_out,
    held,
    peer_slots,
    gather_hot,
    scatter_hot,
    estimate,
    outgoing,
    arrived,
    spread,
    picked,
    tiles,
    high,
    low,
    narrow,
    terms,
    group_terms,
    stacked,
    slot_sums,
    returned,
    load_sem,
    slots_send,
    slots_recv,
    ahead_send,
    ahead_recv,
    tile_send,
    tile_recv,
    term_send,
    term_recv,
    back_send,
    back_recv,
    final_send,
    final_recv,
):
    me, channel = lax.axis_index("vox"), lax.axis_index("chan")
    layer, place = me // PLANE, lax.rem(me, PLANE)
    layers = vox // PLANE
    peers = (2, 1, 3)
    padded, samples, voxels = held.shape
    block_count = model_ref.shape[0]
    rows = tiles.shape[2]
    waves = rows // padded
    pack = 8 // waves
    slot_count = scatter_hot.shape[0]
    f32, bf16 = jnp.float32, jnp.bfloat16

    def chan_peer(step):
        return lax.rem(channel + step, chan)

    barrier = pltpu.get_barrier_semaphore()

    def greet(step, carry):
        peer = lax.rem(me + step, vox)
        pl.semaphore_signal(barrier, inc=1, device_id={"vox": peer}, device_id_type=MESH)
        return carry

    lax.fori_loop(1, vox, greet, 0)
    for p in peers:
        pl.semaphore_signal(barrier, inc=1, device_id={"chan": chan_peer(p)}, device_id_type=MESH)

    load = pltpu.make_async_copy(model_ref, held.at[pl.ds(0, block_count)], load_sem)
    load.start()

    def start_vox(source, target, send_sem, recv_sem, g):
        def send(distance):
            def one(turn, carry):
                for d in distance:
                    peer = lax.rem(layer + d, layers) * PLANE + lax.rem(place + turn, PLANE)
                    pltpu.make_async_remote_copy(
                        src_ref=source.at[g, peer],
                        dst_ref=target.at[g, me],
                        send_sem=send_sem.at[g],
                        recv_sem=recv_sem.at[g],
                        device_id={"vox": peer},
                        device_id_type=MESH,
                    ).start()
                return carry

            return one

        half = layers // 2
        lax.fori_loop(0, PLANE, send((half,)), 0)
        for d in range(half - 1, 0, -1):
            lax.fori_loop(0, PLANE, send((d, layers - d)), 0)
        lax.fori_loop(1, PLANE, send((0,)), 0)
        target[g, me] = source[g, me]

    def wait_vox(source, target, send_sem, recv_sem, g):
        others = pl.ds(0, vox - 1)
        pltpu.make_async_copy(target.at[g, others], target.at[g, others], recv_sem.at[g]).wait()
        pltpu.make_async_copy(source.at[g, others], source.at[g, others], send_sem.at[g]).wait()

    def chan_copy(source, target, send_sem, recv_sem, g, p):
        return pltpu.make_async_remote_copy(
            src_ref=source.at[g, p],
            dst_ref=target.at[g, chan - p],
            send_sem=send_sem.at[g, p],
            recv_sem=recv_sem.at[g, chan - p],
            device_id={"chan": chan_peer(p)},
            device_id_type=MESH,
        )

    def wait_chan(source, target, send_sem, recv_sem, g):
        for p in peers:
            pltpu.make_async_copy(target.at[g, p], target.at[g, p], recv_sem.at[g, p]).wait()
            pltpu.make_async_copy(source.at[g, p], source.at[g, p], send_sem.at[g, p]).wait()

    def start_ahead(g):
        slots = jnp.dot(
            send_hot_ref[...], estimate[g].astype(bf16), preferred_element_type=f32
        )
        outgoing[g] = slots.reshape(outgoing.shape[1:]).astype(bf16)

    def send_ahead(g):
        start_vox(outgoing, arrived, ahead_send, ahead_recv, g)

    def slots_copy(p):
        return pltpu.make_async_remote_copy(
            src_ref=slots_ref,
            dst_ref=peer_slots.at[chan - p],
            send_sem=slots_send.at[p],
            recv_sem=slots_recv.at[chan - p],
            device_id={"chan": chan_peer(p)},
            device_id_type=MESH,
        )

    estimate[...] = start_ref[...]
    for g in range(STREAMS):
        start_ahead(g)
    pl.semaphore_wait(barrier, vox - 1 + chan - 1)
    for p in peers:
        slots_copy(p).start()

    def first_send(g, carry):
        send_ahead(g)
        return carry

    lax.fori_loop(0, STREAMS, first_send, 0)
    held[block_count:] = jnp.zeros((padded - block_count, samples, voxels), bf16)
    stacked[...] = jnp.zeros_like(stacked)
    peer_slots[0] = slots_ref[...]
    for p in peers:
        pltpu.make_async_copy(peer_slots.at[p], peer_slots.at[p], slots_recv.at[p]).wait()
        pltpu.make_async_copy(slots_ref, slots_ref, slots_send.at[p]).wait()
    slot_range = lax.broadcasted_iota(jnp.int32, (slot_count, LANES), 0)
    diagonal_hot = jnp.where(
        lax.broadcasted_iota(jnp.int32, (LANES, LANES), 0)
        == lax.broadcasted_iota(jnp.int32, (LANES, LANES), 1),
        1.0,
        0.0,
    ).astype(bf16)
    for p in range(chan):
        span = slice(p * LANES, (p + 1) * LANES)
        named = jnp.broadcast_to(peer_slots[p][0:1, :], slot_range.shape)
        hot = jnp.where(slot_range == named, 1.0, 0.0).astype(bf16)
        scatter_hot[:, span] = hot
        gather_hot[span, :] = lax.dot_general(
            diagonal_hot, hot, (((1,), (1,)), ((), ())), preferred_element_type=f32
        ).astype(bf16)
    load.wait()

    group_of = lax.broadcasted_iota(jnp.int32, (8, voxels), 0) // waves

    def diagonal(product, p):
        part = slice(8 * p, 8 * p + 8)
        piece = product[part, 0:voxels]
        for i in range(1, pack):
            piece = jnp.where(group_of == i, product[part, i * voxels : (i + 1) * voxels], piece)
        return piece

    def pick_tiles(g):
        wait_vox(outgoing, arrived, ahead_send, ahead_recv, g)
        spread[0 : slot_count * waves, :] = arrived[g].astype(f32).reshape(-1, voxels)
        source = jnp.concatenate(
            [spread[pl.ds(w, slot_count, stride=waves), :] for w in range(waves)], axis=1
        ).astype(bf16)
        product = jnp.dot(gather_hot[...], source, preferred_element_type=f32)
        for p in peers + (0,):
            for w in range(waves):
                spread[pl.ds(p * rows + w, padded, stride=waves), :] = product[
                    p * LANES : p * LANES + padded, w * voxels : (w + 1) * voxels
                ]
            part = spread[p * rows : (p + 1) * rows, :].astype(bf16)
            if p == 0:
                tiles[g, 0] = part
            else:
                picked[g, p] = part
                chan_copy(picked, tiles, tile_send, tile_recv, g, p).start()

    def apply(g):
        wait_chan(picked, tiles, tile_send, tile_recv, g)
        for q in range(rows // 16):
            wide = [tiles[g, p, 16 * q : 16 * q + 16, :].astype(f32) for p in range(chan)]
            halves = []
            for h in range(2):
                left = jnp.concatenate([w[8 * h : 8 * h + 8] for w in wide], axis=0).astype(bf16)
                k = (2 * q + h) * pack
                right = held[k : k + pack].reshape(pack * samples, voxels)
                product = lax.dot_general(
                    left, right, (((1,), (1,)), ((), ())), preferred_element_type=f32
                )
                halves.append([diagonal(product, p) for p in range(chan)])
            for p in range(chan):
                piece = jnp.concatenate([halves[0][p], halves[1][p]], axis=0)
                top = piece.astype(bf16)
                where = slice(p * rows + 16 * q, p * rows + 16 * q + 16)
                high[where, :] = top
                low[where, :] = (piece - top.astype(f32)).astype(bf16)
        predicted = jnp.dot(row_sum_ref[...], high[...], preferred_element_type=f32)
        predicted += jnp.dot(row_sum_ref[...], low[...], preferred_element_type=f32)
        part = predicted.shape[0] // chan
        residuals = []
        for p in range(chan):
            residual = measured_ref[chan_peer(p), g] - predicted[p * part : (p + 1) * part]
            residual_out[chan_peer(p), g] = residual
            residuals.append(residual.astype(bf16))
        if LANES > chan * part:
            residuals.append(jnp.zeros((LANES - chan * part, samples), bf16))
        narrow[...] = jnp.dot(
            row_hot_ref[...], jnp.concatenate(residuals, axis=0), preferred_element_type=f32
        )
        for q in range(rows // 16):
            halves = []
            for h in range(2):
                k = (2 * q + h) * pack
                left = jnp.concatenate(
                    [
                        narrow[p * rows + 16 * q + 8 * h : p * rows + 16 * q + 8 * h + 8, :]
                        for p in range(chan)
                    ],
                    axis=0,
                ).astype(bf16)
                right = jnp.concatenate([held[k + i] for i in range(pack)], axis=1)
                product = jnp.dot(left, right, preferred_element_type=f32)
                halves.append([diagonal(product, p) for p in range(chan)])
            for p in range(chan):
                piece = jnp.concatenate([halves[0][p], halves[1][p]], axis=0).astype(bf16)
                if p == 0:
                    group_terms[g, 0, 16 * q : 16 * q + 16, :] = piece
                else:
                    terms[g, p, 16 * q : 16 * q + 16, :] = piece
        for p in peers:
            chan_copy(terms, group_terms, term_send, term_recv, g, p).start()

    def sum_slots(g):
        wait_chan(terms, group_terms, term_send, term_recv, g)
        for p in range(chan):
            spread[p * rows : (p + 1) * rows, :] = group_terms[g, p].astype(f32)
            for w in range(waves):
                stacked[p * LANES : p * LANES + padded, w * voxels : (w + 1) * voxels] = spread[
                    pl.ds(p * rows + w, padded, stride=waves), :
                ].astype(bf16)
        product = jnp.dot(scatter_hot[...], stacked[...], preferred_element_type=f32)
        for w in range(waves):
            spread[pl.ds(w, slot_count, stride=waves), :] = product[:, w * voxels : (w + 1) * voxels]
        slot_sums[g] = (
            spread[0 : slot_count * waves, :].reshape(slot_sums.shape[1:]).astype(bf16)
        )
        start_vox(slot_sums, returned, back_send, back_recv, g)

    def final_copy(g, p):
        return pltpu.make_async_remote_copy(
            src_ref=estimate.at[g, pl.ds(0, estimate_out.shape[2])],
            dst_ref=estimate_out.at[channel, g],
            send_sem=final_send.at[g, p],
            recv_sem=final_recv.at[g, chan - p],
            device_id={"chan": chan_peer(p)},
            device_id_type=MESH,
        )

    def update(g):
        wait_vox(slot_sums, returned, back_send, back_recv, g)
        gradient = jnp.dot(
            return_hot_ref[...],
            returned[g].astype(f32).reshape(-1, voxels).astype(bf16),
            preferred_element_type=f32,
        )
        estimate[g] = jnp.maximum(estimate[g] + steps_ref[g] * gradient, 0.0)

    turns = ITERATIONS * STREAMS

    def turn(n, carry):
        g = lax.rem(n, STREAMS)

        @pl.when(n < turns)
        def _():
            pick_tiles(g)
            apply(g)

        @pl.when(n >= 1)
        def _():
            other = lax.rem(n + STREAMS - 1, STREAMS)
            update(other)

            @pl.when(n < turns + 1 - STREAMS)
            def _():
                start_ahead(other)
                send_ahead(other)

            @pl.when(n >= turns + 1 - STREAMS)
            def _():
                for p in peers:
                    final_copy(other, p).start()
                estimate_out[channel, other] = estimate[other, 0 : estimate_out.shape[2], :]

        @pl.when(n < turns)
        def _():
            sum_slots(g)

        return carry

    lax.fori_loop(0, turns + 1, turn, 0)

    def finish(g, carry):
        for p in peers:
            landed = estimate_out.at[chan_peer(p), g]
            sent = estimate.at[g, pl.ds(0, estimate_out.shape[2])]
            pltpu.make_async_copy(landed, landed, final_recv.at[g, p]).wait()
            pltpu.make_async_copy(sent, sent, final_send.at[g, p]).wait()
        return carry

    lax.fori_loop(0, STREAMS, finish, 0)


def shards(model_blocks, start_image, measured, step_size, sent_tiles, block_rows, block_slots):
    vox, chan = lax.axis_size("vox"), lax.axis_size("chan")
    channel = lax.axis_index("chan")
    send_table = sent_tiles[0]
    capacity = send_table.shape[1]
    tile_count, wave_count, width = start_image.shape
    row_count, block_count = measured.shape[0], model_blocks.shape[0]
    waves = wave_count // chan // STREAMS
    slots = vox * capacity
    padded = -(-block_count // 16) * 16
    rows = padded * waves
    int32, bf16 = jnp.int32, jnp.bfloat16

    def flat(index, minor):
        spread = index[..., None] * minor + jnp.arange(minor, dtype=int32)
        return jnp.where(index[..., None] < 0, -1, spread).reshape(index.shape[:-1] + (-1,))

    slot_row = jnp.pad(block_slots, (0, LANES - block_count), constant_values=-1)
    slot_row = jnp.broadcast_to(slot_row[None, :], (8, LANES))
    send_code = flat(send_table.reshape(-1), waves)
    tile_range = jnp.arange(LANES)
    send_hot = (send_code[:, None] == tile_range[None, :]).astype(bf16)
    return_hot = (tile_range[:, None] == send_code[None, :]).astype(bf16)
    row_code = jnp.pad(block_rows, (0, padded - block_count), constant_values=-1)
    row_code = jnp.where(
        row_code[None, :] < 0, -1, jnp.arange(chan, dtype=int32)[:, None] * row_count + row_code[None, :]
    )
    row_code = flat(row_code, waves).reshape(-1)
    row_hot = (row_code[:, None] == jnp.arange(LANES)[None, :]).astype(bf16)
    row_sum = (jnp.arange(chan * row_count * waves)[:, None] == row_code[None, :]).astype(bf16)

    own = lax.dynamic_slice_in_dim(start_image, channel * waves * STREAMS, waves * STREAMS, axis=1)
    own = own.reshape(tile_count, STREAMS, waves, width).transpose(1, 0, 2, 3)
    own = own.reshape(STREAMS, tile_count * waves, width)
    own = jnp.pad(own, ((0, 0), (0, LANES - tile_count * waves), (0, 0)))
    steps = lax.dynamic_slice_in_dim(step_size, channel * waves * STREAMS, waves * STREAMS)
    steps = jnp.tile(steps.reshape(STREAMS, waves), (1, LANES // waves))
    steps = jnp.broadcast_to(steps[:, :, None], own.shape)
    split = measured.reshape(row_count, chan, STREAMS, waves, width).transpose(1, 2, 0, 3, 4)
    split = split.reshape(chan, STREAMS, row_count * waves, width)

    packet = (STREAMS, vox, capacity * waves, width)
    quarter = (STREAMS, chan, rows, width)
    dma = pltpu.SemaphoreType.DMA
    estimate, residual = pl.pallas_call(
        functools.partial(landweber_body, vox, chan),
        out_shape=(
            jax.ShapeDtypeStruct((chan, STREAMS, tile_count * waves, width), jnp.float32),
            jax.ShapeDtypeStruct(split.shape, jnp.float32),
        ),
        in_specs=[ANY] + [VMEM] * 8,
        out_specs=(VMEM, VMEM),
        scratch_shapes=[
            pltpu.VMEM((padded,) + model_blocks.shape[1:], bf16),
            pltpu.VMEM((chan,) + slot_row.shape, int32),
            pltpu.VMEM((chan * LANES, slots), bf16),
            pltpu.VMEM((slots, chan * LANES), bf16),
            pltpu.VMEM(own.shape, jnp.float32),
            pltpu.VMEM(packet, bf16),
            pltpu.VMEM(packet, bf16),
            pltpu.VMEM((max(slots * waves, chan * rows), width), jnp.float32),
            pltpu.VMEM(quarter, bf16),
            pltpu.VMEM(quarter, bf16),
            pltpu.VMEM((chan * rows, width), bf16),
            pltpu.VMEM((chan * rows, width), bf16),
            pltpu.VMEM((chan * rows, width), jnp.float32),
            pltpu.VMEM(quarter, bf16),
            pltpu.VMEM(quarter, bf16),
            pltpu.VMEM((chan * LANES, waves * width), bf16),
            pltpu.VMEM(packet, bf16),
            pltpu.VMEM(packet, bf16),
            dma,
            dma((chan,)),
            dma((chan,)),
            dma((STREAMS,)),
            dma((STREAMS,)),
            dma((STREAMS, chan)),
            dma((STREAMS, chan)),
            dma((STREAMS, chan)),
            dma((STREAMS, chan)),
            dma((STREAMS,)),
            dma((STREAMS,)),
            dma((STREAMS, chan)),
            dma((STREAMS, chan)),
        ],
        compiler_params=pltpu.CompilerParams(
            collective_id=0, has_side_effects=True, vmem_limit_bytes=32 << 20
        ),
        name="landweber",
    )(model_blocks, slot_row, own, split, steps, send_hot, return_hot, row_hot, row_sum)
    estimate = estimate.reshape(chan, STREAMS, tile_count, waves, width).transpose(2, 0, 1, 3, 4)
    residual = residual.reshape(chan, STREAMS, row_count, waves, width).transpose(2, 0, 1, 3, 4)
    return (
        estimate.reshape(tile_count, wave_count, width),
        residual.reshape(row_count, wave_count, width),
    )


def solution(mesh):
    in_specs = (
        P(("vox", "chan"), None, None),
        P("vox", None, None),
        P(("vox", "chan"), None, None),
        P(),
        P("vox", None, None),
        P(("vox", "chan")),
        P(("vox", "chan")),
    )
    out_specs = (P("vox", None, None), P(("vox", "chan"), None, None))
    return jax.shard_map(shards, mesh=mesh, in_specs=in_specs, out_specs=out_specs, check_vma=False)
```

time: 198 us -> 211 us (1.066)
  local copies, waits for them, and re-layouts: 4.3 us -> 17.6 us
  starting transfers between devices: 5.28 us -> 0 us
  Pallas kernels: 182 us -> 185 us
    ppermute x3 -> x0, starting transfers between devices: 5.28 us -> none  [shift(): lax.ppermute(value, 'chan', [(c, (c + by) % chan) for c in range(chan)])]
    pallas_call x1, Pallas kernels: 182 us -> 185 us  [shards(): pl.pallas_call(functools.partial(landweber_body, vox, chan), out_shape=(j...]
    unnamed x9 -> x11, local copies, waits for them, and re-layouts: 0.05 us -> 2.75 us
    another operation x3, local copies, waits for them, and re-layouts: 0.19 us -> 2.8 us  [shards(): steps = jnp.tile(steps.reshape(STREAMS, waves), (1, LANES // waves))]
    select_n x4 -> x2, other arithmetic: 0.48 us -> 2.89 us  [flat(): jnp.where(index[..., None] < 0, -1, spread)]
  transfers between devices with their start and end apart: 3 -> 0, of which waited for: 0 -> 0; matrix products, arithmetic and copies ran while one was open for 3% -> 0% of each run, Pallas kernels for 0% -> 0%
where the time goes in v3:
time: 211 us
  Pallas kernels  185 us (88%)
  local copies, waits for them, and re-layouts  17.6 us (8%)
  other arithmetic  7.43 us (4%)
    pallas_call x1, Pallas kernels, shards(): pl.pallas_call(functools.partial(landweber_body, vox, chan), out_shape=(j...  185 us

profile of v3, /device:TPU:1, one launch (start us, length us, event | category | flops | bytes accessed | tf_op | source)
XLA Modules:
  0.0 210.5 jit_solution(2860670280304142985)
XLA Ops:
  0.7 0.8 broadcast_compare_fusion.1
  1.5 0.9 pad.9
  2.4 0.6 fusion.5
  3.0 0.6 fusion.4
  3.6 0.7 dynamic_slice.7
  4.4 0.6 tile.9
  5.0 0.7 pad.8
  5.7 1.2 broadcast_compare_fusion
  6.9 0.7 broadcast_multiply_fusion
  7.5 0.8 copy.15
  8.3 0.6 lt.39
  8.9 0.7 copy.16
  9.6 0.9 mul.42
  10.5 1.3 tile.10
  11.8 0.9 tile.11
  12.7 1.4 add_select_fusion.1
  14.0 1.0 select_n.47
  15.1 0.7 broadcast_in_dim.41.steps_ref
  15.9 0.7 copy.13
  16.6 1.6 copy.14
  18.2 1.5 add_select_fusion
  19.7 1.1 select_n.50
  20.8 0.1 fusion.3.return_hot_ref
  20.8 0.2 fusion.2.send_hot_ref
  21.0 0.1 fusion.1.row_sum_ref
  21.1 0.3 fusion.row_hot_ref
  21.4 0.9 copy-done.2
  22.3 0.9 copy-done.3
  23.2 0.9 copy-done.4
  24.1 184.8 %landweber.1 = (f32[4,2,128,128]{3,2,1,0:T(8,128)S(1)}, f32[4,2,32,128]{3,2,1,0:T(8,128)S(1)}) custom-call(bf16[92,128,128]{2,1,0:T(8,128)(2,1)S(1)} %copy-done.1, s32[8,128]{1,0:T(8,128)S(1)} %broadcast_in_dim.40.slots_ref, f32[2,128,128]{2,1,0:T(8,128)S(1)} %bitcast.16, f32[4,2,32,128]{3,2,1,0:T(8,128)S(1)} %bitcast.17, f32[2,128,128]{2,1,0:T(8,128)S(1)} %copy-done.2, ...), custom_call_target="tpu_custom_call" | custom-call | tf_op jit(solution)/shard_map/landweber/pallas_call | solution.py:399
  208.9 0.9 copy.17
  209.8 0.7 copy.18
  (11 shorter events, 0.1 us)
Async XLA Ops:
  0.6 15.2 %copy-start = (f32[32,32,128]{2,1,0:T(8,128)S(1)}, f32[32,32,128]{2,1,0:T(8,128)}, u32[]{:S(2)}) copy-start(f32[32,32,128]{2,1,0:T(8,128)} %param.8) | copy-start | bytes 1572868
  0.6 20.7 %copy-start.1 = (bf16[92,128,128]{2,1,0:T(8,128)(2,1)S(1)}, bf16[92,128,128]{2,1,0:T(8,128)(2,1)}, u32[]{:S(2)}) copy-start(bf16[92,128,128]{2,1,0:T(8,128)(2,1)} %model_ref.1) | copy-start | bytes 9043972
  21.4 0.9 copy-start.2
  22.3 0.9 copy-start.3
  23.2 0.9 copy-start.4

commit v4 on v3

--- a/solution.py
+++ b/solution.py
@@ -8,7 +8,7 @@
 from jax.sharding import PartitionSpec as P
 
 ITERATIONS = 4
-STREAMS = 2
+STREAMS = 4
 PLANE = 8
 LANES = 128
 MESH = pl.DeviceIdType.MESH
@@ -20,17 +20,20 @@
     vox,
     chan,
     model_ref,
-    slots_ref,
+    codes_ref,
     start_ref,
+    signal_ref,
+    gains_ref,
+    estimate_out,
+    residual_out,
+    held,
+    begin,
     measured_ref,
     steps_ref,
     send_hot_ref,
     return_hot_ref,
     row_hot_ref,
     row_sum_ref,
-    estimate_out,
-    residual_out,
-    held,
     peer_slots,
     gather_hot,
     scatter_hot,
@@ -48,7 +51,7 @@
     stacked,
     slot_sums,
     returned,
-    load_sem,
+    load_sems,
     slots_send,
     slots_recv,
     ahead_send,
@@ -88,7 +91,12 @@
     for p in peers:
         pl.semaphore_signal(barrier, inc=1, device_id={"chan": chan_peer(p)}, device_id_type=MESH)
 
-    load = pltpu.make_async_copy(model_ref, held.at[pl.ds(0, block_count)], load_sem)
+    tile_count, quarter_waves = begin.shape[0], begin.shape[1]
+    row_count = signal_ref.shape[0]
+    own_waves = pl.ds(pl.multiple_of(channel * quarter_waves, quarter_waves), quarter_waves)
+    begin_load = pltpu.make_async_copy(start_ref.at[:, own_waves, :], begin, load_sems.at[0])
+    begin_load.start()
+    load = pltpu.make_async_copy(model_ref, held.at[pl.ds(0, block_count)], load_sems.at[1])
     load.start()
 
     def start_vox(source, target, send_sem, recv_sem, g):
@@ -139,14 +147,18 @@
         slots = jnp.dot(
             send_hot_ref[...], estimate[g].astype(bf16), preferred_element_type=f32
         )
-        outgoing[g] = slots.reshape(outgoing.shape[1:]).astype(bf16)
+        for w in range(waves):
+            spread[pl.ds(w, slot_count, stride=waves), :] = slots[
+                w * slot_count : (w + 1) * slot_count
+            ]
+        outgoing[g] = spread[0 : slot_count * waves, :].reshape(outgoing.shape[1:]).astype(bf16)
 
     def send_ahead(g):
         start_vox(outgoing, arrived, ahead_send, ahead_recv, g)
 
     def slots_copy(p):
         return pltpu.make_async_remote_copy(
-            src_ref=slots_ref,
+            src_ref=codes_ref,
             dst_ref=peer_slots.at[chan - p],
             send_sem=slots_send.at[p],
             recv_sem=slots_recv.at[chan - p],
@@ -154,8 +166,38 @@
             device_id_type=MESH,
         )
 
-    estimate[...] = start_ref[...]
+    def ones_where(condition):
+        return jnp.where(condition, 1.0, 0.0).astype(bf16)
+
+    def iota(shape, dimension):
+        return lax.broadcasted_iota(jnp.int32, shape, dimension)
+
+    diagonal_hot = ones_where(iota((LANES, LANES), 0) == iota((LANES, LANES), 1))
+
+    def turned(hot):
+        return lax.dot_general(
+            diagonal_hot, hot, (((1,), (1,)), ((), ())), preferred_element_type=f32
+        ).astype(bf16)
+
+    for w in range(waves):
+        for part in range(slot_count // LANES):
+            named = jnp.broadcast_to(codes_ref[2 + part : 3 + part, :], (LANES, LANES))
+            target = jnp.where(named < 0, -1, named + w * tile_count)
+            hot = ones_where(iota((LANES, LANES), 0) == target)
+            column = w * slot_count + part * LANES
+            return_hot_ref[:, column : column + LANES] = hot
+            send_hot_ref[column : column + LANES, :] = turned(hot)
+    estimate[...] = jnp.zeros_like(estimate)
+    steps_ref[...] = jnp.zeros_like(steps_ref)
+    begin_load.wait()
     for g in range(STREAMS):
+        for w in range(waves):
+            wave = g * waves + w
+            span = slice(w * tile_count, (w + 1) * tile_count)
+            estimate[g, span, :] = begin[:, wave, :]
+            steps_ref[g, span, :] = jnp.full(
+                (tile_count, voxels), gains_ref[channel * quarter_waves + wave], f32
+            )
         start_ahead(g)
     pl.semaphore_wait(barrier, vox - 1 + chan - 1)
     for p in peers:
@@ -168,25 +210,35 @@
     lax.fori_loop(0, STREAMS, first_send, 0)
     held[block_count:] = jnp.zeros((padded - block_count, samples, voxels), bf16)
     stacked[...] = jnp.zeros_like(stacked)
-    peer_slots[0] = slots_ref[...]
+    peer_slots[0] = codes_ref[...]
     for p in peers:
         pltpu.make_async_copy(peer_slots.at[p], peer_slots.at[p], slots_recv.at[p]).wait()
-        pltpu.make_async_copy(slots_ref, slots_ref, slots_send.at[p]).wait()
-    slot_range = lax.broadcasted_iota(jnp.int32, (slot_count, LANES), 0)
-    diagonal_hot = jnp.where(
-        lax.broadcasted_iota(jnp.int32, (LANES, LANES), 0)
-        == lax.broadcasted_iota(jnp.int32, (LANES, LANES), 1),
-        1.0,
-        0.0,
-    ).astype(bf16)
+        pltpu.make_async_copy(codes_ref, codes_ref, slots_send.at[p]).wait()
+    for q in range(chan):
+        for g in range(STREAMS):
+            for w in range(waves):
+                measured_ref[q, g, w * row_count : (w + 1) * row_count, :] = signal_ref[
+                    :, q * quarter_waves + g * waves + w, :
+                ]
+    lanes = iota((LANES, chan * rows), 1)
+    block_of = lax.div(lax.rem(lanes, rows), waves)
+    row_vector = jnp.broadcast_to(codes_ref[1:2, :], (16, LANES)).astype(f32).astype(bf16)
+    row_lanes = jnp.dot(
+        row_vector, ones_where(iota(lanes.shape, 0) == block_of), preferred_element_type=f32
+    )
+    row_lanes = jnp.broadcast_to(row_lanes[0:1, :], lanes.shape).astype(jnp.int32)
+    target = (lax.div(lanes, rows) * waves + lax.rem(lanes, waves)) * row_count + row_lanes
+    row_sum_ref[...] = ones_where(iota(lanes.shape, 0) == jnp.where(row_lanes < 0, -1, target))
+    for part in range(chan * rows // LANES):
+        span = slice(part * LANES, (part + 1) * LANES)
+        row_hot_ref[span, :] = turned(row_sum_ref[:, span])
+    slot_range = iota((slot_count, LANES), 0)
     for p in range(chan):
         span = slice(p * LANES, (p + 1) * LANES)
         named = jnp.broadcast_to(peer_slots[p][0:1, :], slot_range.shape)
-        hot = jnp.where(slot_range == named, 1.0, 0.0).astype(bf16)
+        hot = ones_where(slot_range == named)
         scatter_hot[:, span] = hot
-        gather_hot[span, :] = lax.dot_general(
-            diagonal_hot, hot, (((1,), (1,)), ((), ())), preferred_element_type=f32
-        ).astype(bf16)
+        gather_hot[span, :] = turned(hot)
     load.wait()
 
     group_of = lax.broadcasted_iota(jnp.int32, (8, voxels), 0) // waves
@@ -238,14 +290,13 @@
                 low[where, :] = (piece - top.astype(f32)).astype(bf16)
         predicted = jnp.dot(row_sum_ref[...], high[...], preferred_element_type=f32)
         predicted += jnp.dot(row_sum_ref[...], low[...], preferred_element_type=f32)
-        part = predicted.shape[0] // chan
+        part = waves * row_count
         residuals = []
         for p in range(chan):
             residual = measured_ref[chan_peer(p), g] - predicted[p * part : (p + 1) * part]
             residual_out[chan_peer(p), g] = residual
             residuals.append(residual.astype(bf16))
-        if LANES > chan * part:
-            residuals.append(jnp.zeros((LANES - chan * part, samples), bf16))
+        residuals.append(jnp.zeros((LANES - chan * part, samples), bf16))
         narrow[...] = jnp.dot(
             row_hot_ref[...], jnp.concatenate(residuals, axis=0), preferred_element_type=f32
         )
@@ -300,9 +351,13 @@
 
     def update(g):
         wait_vox(slot_sums, returned, back_send, back_recv, g)
+        spread[0 : slot_count * waves, :] = returned[g].astype(f32).reshape(-1, voxels)
+        source = jnp.concatenate(
+            [spread[pl.ds(w, slot_count, stride=waves), :] for w in range(waves)], axis=0
+        ).astype(bf16)
         gradient = jnp.dot(
             return_hot_ref[...],
-            returned[g].astype(f32).reshape(-1, voxels).astype(bf16),
+            source,
             preferred_element_type=f32,
         )
         estimate[g] = jnp.maximum(estimate[g] + steps_ref[g] * gradient, 0.0)
@@ -310,36 +365,37 @@
     turns = ITERATIONS * STREAMS
 
     def turn(n, carry):
-        g = lax.rem(n, STREAMS)
-
         @pl.when(n < turns)
         def _():
-            pick_tiles(g)
-            apply(g)
-
-        @pl.when(n >= 1)
+            pick_tiles(lax.rem(n, STREAMS))
+
+        @pl.when((n >= 1) & (n < turns + 1))
         def _():
-            other = lax.rem(n + STREAMS - 1, STREAMS)
-            update(other)
-
-            @pl.when(n < turns + 1 - STREAMS)
+            sum_slots(lax.rem(n + STREAMS - 1, STREAMS))
+
+        @pl.when(n < turns)
+        def _():
+            apply(lax.rem(n, STREAMS))
+
+        @pl.when(n >= 2)
+        def _():
+            g = lax.rem(n + STREAMS - 2, STREAMS)
+            update(g)
+
+            @pl.when(n < turns + 2 - STREAMS)
             def _():
-                start_ahead(other)
-                send_ahead(other)
-
-            @pl.when(n >= turns + 1 - STREAMS)
+                start_ahead(g)
+                send_ahead(g)
+
+            @pl.when(n >= turns + 2 - STREAMS)
             def _():
                 for p in peers:
-                    final_copy(other, p).start()
-                estimate_out[channel, other] = estimate[other, 0 : estimate_out.shape[2], :]
-
-        @pl.when(n < turns)
-        def _():
-            sum_slots(g)
+                    final_copy(g, p).start()
+                estimate_out[channel, g] = estimate[g, 0 : estimate_out.shape[2], :]
 
         return carry
 
-    lax.fori_loop(0, turns + 1, turn, 0)
+    lax.fori_loop(0, turns + 2, turn, 0)
 
     def finish(g, carry):
         for p in peers:
@@ -354,7 +410,6 @@
 
 def shards(model_blocks, start_image, measured, step_size, sent_tiles, block_rows, block_slots):
     vox, chan = lax.axis_size("vox"), lax.axis_size("chan")
-    channel = lax.axis_index("chan")
     send_table = sent_tiles[0]
     capacity = send_table.shape[1]
     tile_count, wave_count, width = start_image.shape
@@ -365,34 +420,14 @@
     rows = padded * waves
     int32, bf16 = jnp.int32, jnp.bfloat16
 
-    def flat(index, minor):
-        spread = index[..., None] * minor + jnp.arange(minor, dtype=int32)
-        return jnp.where(index[..., None] < 0, -1, spread).reshape(index.shape[:-1] + (-1,))
-
-    slot_row = jnp.pad(block_slots, (0, LANES - block_count), constant_values=-1)
-    slot_row = jnp.broadcast_to(slot_row[None, :], (8, LANES))
-    send_code = flat(send_table.reshape(-1), waves)
-    tile_range = jnp.arange(LANES)
-    send_hot = (send_code[:, None] == tile_range[None, :]).astype(bf16)
-    return_hot = (tile_range[:, None] == send_code[None, :]).astype(bf16)
-    row_code = jnp.pad(block_rows, (0, padded - block_count), constant_values=-1)
-    row_code = jnp.where(
-        row_code[None, :] < 0, -1, jnp.arange(chan, dtype=int32)[:, None] * row_count + row_code[None, :]
+    codes = jnp.pad(
+        jnp.stack([block_slots, block_rows]), ((0, 0), (0, LANES - block_count)), constant_values=-1
     )
-    row_code = flat(row_code, waves).reshape(-1)
-    row_hot = (row_code[:, None] == jnp.arange(LANES)[None, :]).astype(bf16)
-    row_sum = (jnp.arange(chan * row_count * waves)[:, None] == row_code[None, :]).astype(bf16)
-
-    own = lax.dynamic_slice_in_dim(start_image, channel * waves * STREAMS, waves * STREAMS, axis=1)
-    own = own.reshape(tile_count, STREAMS, waves, width).transpose(1, 0, 2, 3)
-    own = own.reshape(STREAMS, tile_count * waves, width)
-    own = jnp.pad(own, ((0, 0), (0, LANES - tile_count * waves), (0, 0)))
-    steps = lax.dynamic_slice_in_dim(step_size, channel * waves * STREAMS, waves * STREAMS)
-    steps = jnp.tile(steps.reshape(STREAMS, waves), (1, LANES // waves))
-    steps = jnp.broadcast_to(steps[:, :, None], own.shape)
-    split = measured.reshape(row_count, chan, STREAMS, waves, width).transpose(1, 2, 0, 3, 4)
-    split = split.reshape(chan, STREAMS, row_count * waves, width)
-
+    table = send_table.reshape(slots // LANES, LANES)
+    codes = jnp.concatenate([codes, table, jnp.zeros((6 - slots // LANES, LANES), int32)])
+
+    signals = (chan, STREAMS, waves * row_count, width)
+    estimates = (STREAMS, LANES, width)
     packet = (STREAMS, vox, capacity * waves, width)
     quarter = (STREAMS, chan, rows, width)
     dma = pltpu.SemaphoreType.DMA
@@ -400,16 +435,23 @@
         functools.partial(landweber_body, vox, chan),
         out_shape=(
             jax.ShapeDtypeStruct((chan, STREAMS, tile_count * waves, width), jnp.float32),
-            jax.ShapeDtypeStruct(split.shape, jnp.float32),
+            jax.ShapeDtypeStruct(signals, jnp.float32),
         ),
-        in_specs=[ANY] + [VMEM] * 8,
+        in_specs=[ANY, VMEM, ANY, VMEM, pl.BlockSpec(memory_space=pltpu.SMEM)],
         out_specs=(VMEM, VMEM),
         scratch_shapes=[
             pltpu.VMEM((padded,) + model_blocks.shape[1:], bf16),
-            pltpu.VMEM((chan,) + slot_row.shape, int32),
+            pltpu.VMEM((tile_count, wave_count // chan, width), jnp.float32),
+            pltpu.VMEM(signals, jnp.float32),
+            pltpu.VMEM(estimates, jnp.float32),
+            pltpu.VMEM((slots * waves, LANES), bf16),
+            pltpu.VMEM((LANES, slots * waves), bf16),
+            pltpu.VMEM((chan * rows, LANES), bf16),
+            pltpu.VMEM((LANES, chan * rows), bf16),
+            pltpu.VMEM((chan,) + codes.shape, int32),
             pltpu.VMEM((chan * LANES, slots), bf16),
             pltpu.VMEM((slots, chan * LANES), bf16),
-            pltpu.VMEM(own.shape, jnp.float32),
+            pltpu.VMEM(estimates, jnp.float32),
             pltpu.VMEM(packet, bf16),
             pltpu.VMEM(packet, bf16),
             pltpu.VMEM((max(slots * waves, chan * rows), width), jnp.float32),
@@ -423,7 +465,7 @@
             pltpu.VMEM((chan * LANES, waves * width), bf16),
             pltpu.VMEM(packet, bf16),
             pltpu.VMEM(packet, bf16),
-            dma,
+            dma((2,)),
             dma((chan,)),
             dma((chan,)),
             dma((STREAMS,)),
@@ -441,9 +483,9 @@
             collective_id=0, has_side_effects=True, vmem_limit_bytes=32 << 20
         ),
         name="landweber",
-    )(model_blocks, slot_row, own, split, steps, send_hot, return_hot, row_hot, row_sum)
-    estimate = estimate.reshape(chan, STREAMS, tile_count, waves, width).transpose(2, 0, 1, 3, 4)
-    residual = residual.reshape(chan, STREAMS, row_count, waves, width).transpose(2, 0, 1, 3, 4)
+    )(model_blocks, codes, start_image, measured, step_size)
+    estimate = estimate.reshape(chan, STREAMS, waves, tile_count, width).transpose(3, 0, 1, 2, 4)
+    residual = residual.reshape(chan, STREAMS, waves, row_count, width).transpose(3, 0, 1, 2, 4)
     return (
         estimate.reshape(tile_count, wave_count, width),
         residual.reshape(row_count, wave_count, width),

time: 211 us -> 176 us (0.83)
  Pallas kernels: 185 us -> 167 us
  local copies, waits for them, and re-layouts: 17.6 us -> 7.33 us
  other arithmetic: 7.43 us -> 0.75 us
    pallas_call x1, Pallas kernels: 185 us -> 167 us  [shards(): pl.pallas_call(functools.partial(landweber_body, vox, chan), out_shape=(j...]
    select_n x2 -> x0, other arithmetic: 2.89 us -> none  [flat(): jnp.where(index[..., None] < 0, -1, spread)]
    another operation x3 -> x1, local copies, waits for them, and re-layouts: 2.8 us -> 0.1 us  [shards(): table = send_table.reshape(slots // LANES, LANES)]
    lt x3 -> x0, other arithmetic: 2.63 us -> none  [the longest x2 1.81 us: flat(): index[..., None] < 0]
    unnamed x11 -> x9, local copies, waits for them, and re-layouts: 2.75 us -> 5.23 us
where the time goes in v4:
time: 176 us; the launch traced here: 175 us
  Pallas kernels  167 us (95%)
  local copies, waits for them, and re-layouts  7.33 us (4%)
    pallas_call x1, Pallas kernels, shards(): pl.pallas_call(functools.partial(landweber_body, vox, chan), out_shape=(j...  167 us
    unnamed x9, local copies, waits for them, and re-layouts  5.23 us

profile of v4, /device:TPU:1, one launch (start us, length us, event | category | flops | bytes accessed | tf_op | source)
XLA Modules:
  0.0 175.4 jit_solution(16566101659337275305)
XLA Ops:
  0.6 0.1 pad.7.clone
  0.7 0.7 pad_add_fusion
  1.4 0.8 copy.12
  2.2 0.1 reshape_squeeze.3
  2.3 0.1 fusion.codes_ref
  2.3 0.0 copy-start
  2.3 1.9 %copy-done = bf16[92,128,128]{2,1,0:T(8,128)(2,1)S(1)} copy-done((bf16[92,128,128]{2,1,0:T(8,128)(2,1)S(1)}, bf16[92,128,128]{2,1,0:T(8,128)(2,1)}, u32[]{:S(2)}) %copy-start) | copy-done | bytes 3014680
  4.2 0.0 copy-start.1
  4.2 1.0 copy-done.1
  5.2 0.0 copy-start.2
  5.2 0.9 copy-done.2
  6.1 0.0 copy-start.3
  6.1 0.7 copy-done.3
  6.8 166.7 %landweber.1 = (f32[4,4,64,128]{3,2,1,0:T(8,128)S(1)}, f32[4,4,16,128]{3,2,1,0:T(8,128)S(1)}) custom-call(bf16[92,128,128]{2,1,0:T(8,128)(2,1)S(1)} %copy-done, s32[8,128]{1,0:T(8,128)S(1)} %fusion.codes_ref, f32[32,32,128]{2,1,0:T(8,128)S(1)} %copy-done.1, f32[8,32,128]{2,1,0:T(8,128)S(1)} %copy-done.2, f32[32]{0:T(128)S(1)} %copy-done.3), custom_call_target="tpu_custom_call" | custom-call | tf_op jit(solution)/shard_map/landweber/pallas_call | solution.py:434
  173.5 1.2 copy.13
  174.7 0.7 copy.14
  (1 shorter events, 0.0 us)
Async XLA Ops:
  2.3 1.9 %copy-start = (bf16[92,128,128]{2,1,0:T(8,128)(2,1)S(1)}, bf16[92,128,128]{2,1,0:T(8,128)(2,1)}, u32[]{:S(2)}) copy-start(bf16[92,128,128]{2,1,0:T(8,128)(2,1)} %model_ref.1) | copy-start | bytes 9043972
  4.2 1.0 copy-start.1
  5.2 0.9 copy-start.2
  6.1 0.7 copy-start.3
